TPU v7x, 32 devices: a whole 2x2x4 slice. The times are simulated.
32 devices in a mesh: dp: 8 (over z, x), tensor: 4 (over y, core).
Axes of the slice: x: 2, y: 2, z: 4, core: 2. Of those that a mesh axis runs over, the one named last changes fastest.
Arguments:
- patches: bfloat16 [16384, 768], P(('dp', 'tensor')), may hold values from -6 to 6
- cotangent: bfloat16 [16384, 768], P(('dp', 'tensor')), may hold values from -6 to 6
- mask_rows: int32 [16384], P(('dp', 'tensor')), may hold values 0 or 1
- count_big: int32 [8], P('dp'), may hold values from 0 to 10
- pos_big: bfloat16 [197, 768], replicated, may hold values from -4 to 4
- pos_small: bfloat16 [101, 768], replicated, may hold values from -4 to 4
- step_count: int32 [1], replicated, may hold values from 1 to 20
- qkv_master: float32 [3, 768, 768], P(None, 'dp', 'tensor'), may hold values from -0.21875 to 0.21875
- qkv_first: float32 [3, 768, 768], P(None, 'dp', 'tensor')
- qkv_second: float32 [3, 768, 768], P(None, 'dp', 'tensor'), as said below
- out_master: float32 [768, 768], P('tensor', 'dp'), may hold values from -0.875 to 0.875
- out_first: float32 [768, 768], P('tensor', 'dp')
- out_second: float32 [768, 768], P('tensor', 'dp'), as said below
- up_master: float32 [768, 3072], P('dp', 'tensor'), may hold values from -0.21875 to 0.21875
- up_first: float32 [768, 3072], P('dp', 'tensor')
- up_second: float32 [768, 3072], P('dp', 'tensor'), as said below
- down_master: float32 [3072, 768], P('tensor', 'dp'), may hold values from -0.109375 to 0.109375
- down_first: float32 [3072, 768], P('tensor', 'dp')
- down_second: float32 [3072, 768], P('tensor', 'dp'), as said below
- norm_gains: float32 [4, 768], replicated, may hold values from 0.25 to 1.75
- gain_first: float32 [4, 768], replicated
- gain_second: float32 [4, 768], replicated, as said below
- shifts: float32 [11, 768], replicated, may hold values from -3 to 3
- shift_first: float32 [11, 768], replicated
- shift_second: float32 [11, 768], replicated, as said below
Outputs:
- layer_out: bfloat16 [16384, 768], P(('dp', 'tensor'))
- patch_grad: float32 [16384, 768], P(('dp', 'tensor'))
- qkv_new: float32 [3, 768, 768], P(None, 'dp', 'tensor')
- qkv_first_new: float32 [3, 768, 768], P(None, 'dp', 'tensor')
- qkv_second_new: float32 [3, 768, 768], P(None, 'dp', 'tensor')
- qkv_copy: bfloat16 [3, 768, 768], P(None, 'dp', 'tensor')
- out_new: float32 [768, 768], P('tensor', 'dp')
- out_first_new: float32 [768, 768], P('tensor', 'dp')
- out_second_new: float32 [768, 768], P('tensor', 'dp')
- out_copy: bfloat16 [768, 768], P('tensor', 'dp')
- up_new: float32 [768, 3072], P('dp', 'tensor')
- up_first_new: float32 [768, 3072], P('dp', 'tensor')
- up_second_new: float32 [768, 3072], P('dp', 'tensor')
- up_copy: bfloat16 [768, 3072], P('dp', 'tensor')
- down_new: float32 [3072, 768], P('tensor', 'dp')
- down_first_new: float32 [3072, 768], P('tensor', 'dp')
- down_second_new: float32 [3072, 768], P('tensor', 'dp')
- down_copy: bfloat16 [3072, 768], P('tensor', 'dp')
- gain_new: float32 [4, 768], replicated
- gain_first_new: float32 [4, 768], replicated
- gain_second_new: float32 [4, 768], replicated
- gain_copy: bfloat16 [4, 768], replicated
- shift_new: float32 [11, 768], replicated
- shift_first_new: float32 [11, 768], replicated
- shift_second_new: float32 [11, 768], replicated
- shift_copy: bfloat16 [11, 768], replicated
Inputs may be any that keep to these rules, and one draw needn't show every extreme that they name: `qkv_second`: every entry is positive. `out_second`: every entry is positive. `up_second`: every entry is positive. `down_second`: every entry is positive. `gain_second`: every entry is positive. `shift_second`: every entry is positive.
All inputs are finite; a program needn't handle non-finite values. No bound on the sum of `mask_rows` on one device may be relied on, other than what follows from the above.
Results may differ from a plain program's by a relative error of at most 0.012.
The roundings to bfloat16 on the way count: a program that leaves them out, or rounds other values in their place, can miss the bound.
Values may be sent and summed in bfloat16 or wider, within the bound.
No kernel may reach another device: no remote copies, remote signals or barrier semaphores. Data moves between devices by JAX's collectives and lax.ppermute only.
A program may use at most 128 MiB of HBM per device.

v0:
```python
import jax
import jax.numpy as jnp
from jax import lax
from jax.sharding import PartitionSpec as P

D = 768
HEAD_DIM = 64
FF = 3072
BIG_LEN = 197
SMALL_LEN = 101
QBLOCK = 512
MARGIN = 256


EPS_NORM = 1e-06
ADAM_EPS = 1e-08
DECAY = 0.05
NEGATIVE = -1e30


def row_layout(count_big, total_rows):
    row_ids = jnp.arange(total_rows, dtype=jnp.int32)
    big_rows = count_big * BIG_LEN
    count_small = (total_rows - big_rows) // SMALL_LEN
    used_rows = big_rows + count_small * SMALL_LEN
    remainder = row_ids - big_rows
    is_big = row_ids < big_rows
    is_valid = row_ids < used_rows
    segment = jnp.where(is_big, row_ids // BIG_LEN, count_big + remainder // SMALL_LEN)
    segment = jnp.where(is_valid, segment, -1)
    position = jnp.where(is_big, row_ids % BIG_LEN, remainder % SMALL_LEN)
    is_small = is_valid & jnp.logical_not(is_big)
    return (segment, position, is_big, is_small, is_valid)


def contract_rows(left_rows, right_rows):
    return lax.dot_general(
        left_rows, right_rows, (((0,), (0,)), ((), ())), preferred_element_type=jnp.float32
    )


def times_transposed(left_rows, matrix):
    return lax.dot_general(
        left_rows, matrix, (((1,), (1,)), ((), ())), preferred_element_type=jnp.float32
    )


def exact_gelu(values):
    return jax.nn.gelu(values, approximate=False)


def norm_parts(values, gain, shift):
    average = jnp.mean(values, axis=-1, keepdims=True)
    centered = values - average
    inverse = lax.rsqrt(jnp.mean(centered * centered, axis=-1, keepdims=True) + EPS_NORM)
    normal_rows = centered * inverse
    return (normal_rows * gain + shift, normal_rows, inverse)


def norm_back(grad_rows, normal_rows, inverse, gain):
    scaled = grad_rows * gain
    return inverse * (
        scaled
        - jnp.mean(scaled, axis=-1, keepdims=True)
        - normal_rows * jnp.mean(scaled * normal_rows, axis=-1, keepdims=True)
    )


def window_scores(query_rows, key_rows, seg_query, seg_key, head_count):
    block_rows = query_rows.shape[0]
    window = key_rows.shape[0]
    scores = jnp.einsum(
        "qhd,khd->hqk",
        query_rows.reshape(block_rows, head_count, HEAD_DIM),
        key_rows.reshape(window, head_count, HEAD_DIM),
        preferred_element_type=jnp.float32,
    ) * HEAD_DIM ** (-0.5)
    same_image = seg_query[:, None] == seg_key[None, :]
    return jnp.where(same_image[None], scores, NEGATIVE)


def attention_forward(queries, key_all, value_all, segment, head_count):
    total_rows = queries.shape[0]
    lanes = queries.shape[1]
    width_keys = QBLOCK + 2 * MARGIN
    keys_pad = jnp.pad(key_all, ((MARGIN, MARGIN), (0, 0)))
    values_pad = jnp.pad(value_all, ((MARGIN, MARGIN), (0, 0)))
    seg_pad = jnp.pad(segment, (MARGIN, MARGIN), constant_values=-2)

    def one_block(block_id):
        offset = block_id * QBLOCK
        scores = window_scores(
            lax.dynamic_slice_in_dim(queries, offset, QBLOCK),
            lax.dynamic_slice_in_dim(keys_pad, offset, width_keys),
            lax.dynamic_slice_in_dim(segment, offset, QBLOCK),
            lax.dynamic_slice_in_dim(seg_pad, offset, width_keys),
            head_count,
        )
        highest = jnp.max(scores, axis=-1, keepdims=True)
        exp_scores = jnp.exp(scores - highest)
        totals = jnp.sum(exp_scores, axis=-1, keepdims=True)
        weight_low = (exp_scores / totals).astype(jnp.bfloat16)
        value_rows = lax.dynamic_slice_in_dim(values_pad, offset, width_keys).reshape(
            width_keys, head_count, HEAD_DIM
        )
        mixed = jnp.einsum(
            "hqk,khd->qhd", weight_low, value_rows, preferred_element_type=jnp.float32
        )
        return (
            mixed.reshape(QBLOCK, lanes).astype(jnp.bfloat16),
            highest[..., 0] + jnp.log(totals[..., 0]),
        )

    mixed_blocks, log_totals = lax.map(one_block, jnp.arange(total_rows // QBLOCK))
    return (mixed_blocks.reshape(total_rows, lanes), log_totals)


def attention_backward(queries, key_all, value_all, grad_mixed, segment, log_totals, head_count):
    total_rows = queries.shape[0]
    lanes = queries.shape[1]
    width_keys = QBLOCK + 2 * MARGIN
    keys_pad = jnp.pad(key_all, ((MARGIN, MARGIN), (0, 0)))
    values_pad = jnp.pad(value_all, ((MARGIN, MARGIN), (0, 0)))
    seg_pad = jnp.pad(segment, (MARGIN, MARGIN), constant_values=-2)
    factor = HEAD_DIM ** (-0.5)

    def one_block(carry, block_id):
        grad_keys, grad_values = carry
        offset = block_id * QBLOCK
        query_rows = lax.dynamic_slice_in_dim(queries, offset, QBLOCK)
        key_rows = lax.dynamic_slice_in_dim(keys_pad, offset, width_keys)
        value_rows = lax.dynamic_slice_in_dim(values_pad, offset, width_keys).reshape(
            width_keys, head_count, HEAD_DIM
        )
        grad_rows = lax.dynamic_slice_in_dim(grad_mixed, offset, QBLOCK).reshape(
            QBLOCK, head_count, HEAD_DIM
        )
        scores = window_scores(
            query_rows,
            key_rows,
            lax.dynamic_slice_in_dim(segment, offset, QBLOCK),
            lax.dynamic_slice_in_dim(seg_pad, offset, width_keys),
            head_count,
        )
        probs = jnp.exp(scores - log_totals[block_id][:, :, None])
        grad_probs = jnp.einsum(
            "qhd,khd->hqk", grad_rows, value_rows, preferred_element_type=jnp.float32
        )
        inner = jnp.sum(probs * grad_probs, axis=-1, keepdims=True)
        grad_scores = (probs * (grad_probs - inner)).astype(jnp.bfloat16)
        grad_query = (
            jnp.einsum(
                "hqk,khd->qhd",
                grad_scores,
                key_rows.reshape(width_keys, head_count, HEAD_DIM),
                preferred_element_type=jnp.float32,
            )
            * factor
        )
        grad_key = (
            jnp.einsum(
                "hqk,qhd->khd",
                grad_scores,
                query_rows.reshape(QBLOCK, head_count, HEAD_DIM),
                preferred_element_type=jnp.float32,
            )
            * factor
        )
        grad_value = jnp.einsum(
            "hqk,qhd->khd",
            probs.astype(jnp.bfloat16),
            grad_rows,
            preferred_element_type=jnp.float32,
        )
        grad_keys = lax.dynamic_update_slice_in_dim(
            grad_keys,
            lax.dynamic_slice_in_dim(grad_keys, offset, width_keys)
            + grad_key.reshape(width_keys, lanes),
            offset,
            0,
        )
        grad_values = lax.dynamic_update_slice_in_dim(
            grad_values,
            lax.dynamic_slice_in_dim(grad_values, offset, width_keys)
            + grad_value.reshape(width_keys, lanes),
            offset,
            0,
        )
        return ((grad_keys, grad_values), grad_query.reshape(QBLOCK, lanes).astype(jnp.bfloat16))

    zero_pad = jnp.zeros((total_rows + 2 * MARGIN, lanes), jnp.float32)
    (grad_keys, grad_values), grad_blocks = lax.scan(
        one_block, (zero_pad, zero_pad), jnp.arange(total_rows // QBLOCK)
    )
    grad_q = grad_blocks.reshape(total_rows, lanes)
    grad_k = grad_keys[MARGIN : MARGIN + total_rows].astype(jnp.bfloat16)
    grad_v = grad_values[MARGIN : MARGIN + total_rows].astype(jnp.bfloat16)
    return (grad_q, grad_k, grad_v)


def adamw_step(master, first, second, gradient, rate, decay, correction):
    first_new = 0.5 * first + 0.5 * gradient
    second_new = 0.5 * second + 0.5 * gradient * gradient
    update = first_new / correction / (jnp.sqrt(second_new / correction) + ADAM_EPS)
    master_new = master - rate * (update + decay * master)
    return (master_new, first_new, second_new, master_new.astype(jnp.bfloat16))


def on_device(
    patches,
    cotangent,
    mask_rows,
    count_big,
    pos_big,
    pos_small,
    step_count,
    qkv_master,
    qkv_first,
    qkv_second,
    out_master,
    out_first,
    out_second,
    up_master,
    up_first,
    up_second,
    down_master,
    down_first,
    down_second,
    norm_gains,
    gain_first,
    gain_second,
    shifts,
    shift_first,
    shift_second,
):
    tensor_size = lax.axis_size("tensor")
    tensor_id = lax.axis_index("tensor")
    local_rows = patches.shape[0]
    total_rows = local_rows * tensor_size
    width = patches.shape[1]
    lanes = qkv_master.shape[2]
    hidden_lanes = up_master.shape[1]
    head_count = lanes // HEAD_DIM
    segment, position, is_big, is_small, is_valid = row_layout(count_big[0], total_rows)
    own_start = tensor_id * local_rows
    pos_local = lax.dynamic_slice_in_dim(position, own_start, local_rows)
    big_local = lax.dynamic_slice_in_dim(is_big, own_start, local_rows)
    small_local = lax.dynamic_slice_in_dim(is_small, own_start, local_rows)
    valid_local = lax.dynamic_slice_in_dim(is_valid, own_start, local_rows)
    masked = (mask_rows == 1) & valid_local
    qkv_w, out_w, up_w, down_w = (
        lax.all_gather(qkv_master.astype(jnp.bfloat16), "dp", axis=1, tiled=True),
        lax.all_gather(out_master.astype(jnp.bfloat16), "dp", axis=1, tiled=True),
        lax.all_gather(up_master.astype(jnp.bfloat16), "dp", axis=0, tiled=True),
        lax.all_gather(down_master.astype(jnp.bfloat16), "dp", axis=1, tiled=True),
    )
    pick_big = (
        (pos_local[:, None] == jnp.arange(BIG_LEN, dtype=jnp.int32)[None, :]) & big_local[:, None]
    ).astype(jnp.bfloat16)
    pick_small = (
        (pos_local[:, None] == jnp.arange(SMALL_LEN, dtype=jnp.int32)[None, :])
        & small_local[:, None]
    ).astype(jnp.bfloat16)
    placed = jnp.dot(pick_big, pos_big, preferred_element_type=jnp.float32) + jnp.dot(
        pick_small, pos_small, preferred_element_type=jnp.float32
    )
    start_rows = (
        jnp.where(masked[:, None], shifts[6][None, :], patches.astype(jnp.float32)) + placed
    )
    query_bias = lax.dynamic_slice_in_dim(shifts[1], tensor_id * lanes, lanes)
    value_bias = lax.dynamic_slice_in_dim(shifts[2], tensor_id * lanes, lanes)
    up_bias = lax.dynamic_slice_in_dim(
        shifts[7:].reshape(-1), tensor_id * hidden_lanes, hidden_lanes
    )
    normed, normal_one, inverse_one = norm_parts(start_rows, norm_gains[0], shifts[0])
    rows_piece = lax.all_gather(normed.astype(jnp.bfloat16), "tensor", axis=0, tiled=True)
    query_part = jnp.dot(rows_piece, qkv_w[0], preferred_element_type=jnp.float32) + query_bias
    key_part = jnp.dot(rows_piece, qkv_w[1], preferred_element_type=jnp.float32)
    value_part = jnp.dot(rows_piece, qkv_w[2], preferred_element_type=jnp.float32) + value_bias
    queries = query_part.astype(jnp.bfloat16)
    key_all = key_part.astype(jnp.bfloat16)
    value_all = value_part.astype(jnp.bfloat16)
    normed_all = rows_piece
    mixed_all, log_totals = attention_forward(queries, key_all, value_all, segment, head_count)
    branch_attn = (
        lax.psum_scatter(
            jnp.dot(mixed_all, out_w, preferred_element_type=jnp.float32),
            "tensor",
            scatter_dimension=0,
            tiled=True,
        )
        + shifts[3]
    )
    middle = start_rows + norm_gains[2] * branch_attn
    normed_two, normal_two, inverse_two = norm_parts(middle, norm_gains[1], shifts[4])
    rows_piece = lax.all_gather(normed_two.astype(jnp.bfloat16), "tensor", axis=0, tiled=True)
    pre_all = jnp.dot(rows_piece, up_w, preferred_element_type=jnp.float32) + up_bias
    normed_two_all = rows_piece
    hidden_all = exact_gelu(pre_all).astype(jnp.bfloat16)
    branch_mlp = (
        lax.psum_scatter(
            jnp.dot(hidden_all, down_w, preferred_element_type=jnp.float32).astype(jnp.bfloat16),
            "tensor",
            scatter_dimension=0,
            tiled=True,
        ).astype(jnp.float32)
        + shifts[5]
    )
    layer_out = (middle + norm_gains[3] * branch_mlp).astype(jnp.bfloat16)
    qkv_w, out_w, up_w, down_w = (
        lax.all_gather(qkv_master.astype(jnp.bfloat16), "dp", axis=1, tiled=True),
        lax.all_gather(out_master.astype(jnp.bfloat16), "dp", axis=1, tiled=True),
        lax.all_gather(up_master.astype(jnp.bfloat16), "dp", axis=0, tiled=True),
        lax.all_gather(down_master.astype(jnp.bfloat16), "dp", axis=1, tiled=True),
    )
    grad_out = cotangent.astype(jnp.float32) * valid_local[:, None].astype(jnp.float32)
    scale_two_grad = jnp.sum(grad_out * branch_mlp, axis=0)
    grad_branch = (norm_gains[3] * grad_out).astype(jnp.bfloat16)
    down_bias_grad = jnp.sum(grad_branch.astype(jnp.float32), axis=0)
    rows_piece = lax.all_gather(grad_branch, "tensor", axis=0, tiled=True)
    grad_down = contract_rows(hidden_all, rows_piece)
    grad_hidden = times_transposed(rows_piece, down_w)
    gelu_pull = jax.vjp(exact_gelu, pre_all)[1]
    pre_grad = gelu_pull(grad_hidden)[0].astype(jnp.bfloat16)
    up_grad = contract_rows(normed_two_all, pre_grad)
    up_bias_part = jnp.sum(pre_grad.astype(jnp.float32), axis=0)
    grad_normed_two = lax.psum_scatter(
        times_transposed(pre_grad, up_w), "tensor", scatter_dimension=0, tiled=True
    )
    ln_two_gain_grad = jnp.sum(grad_normed_two * normal_two, axis=0)
    ln_two_bias_grad = jnp.sum(grad_normed_two, axis=0)
    grad_middle = grad_out + norm_back(grad_normed_two, normal_two, inverse_two, norm_gains[1])
    scale_one_grad = jnp.sum(grad_middle * branch_attn, axis=0)
    grad_attn = (norm_gains[2] * grad_middle).astype(jnp.bfloat16)
    out_bias_grad = jnp.sum(grad_attn.astype(jnp.float32), axis=0)
    rows_piece = lax.all_gather(grad_attn, "tensor", axis=0, tiled=True)
    grad_outw = contract_rows(mixed_all, rows_piece)
    mix_rows = times_transposed(rows_piece, out_w).astype(jnp.bfloat16)
    grad_q, grad_k, grad_v = attention_backward(
        queries, key_all, value_all, mix_rows, segment, log_totals, head_count
    )
    qkv_grad = jnp.stack(
        [
            contract_rows(normed_all, grad_q),
            contract_rows(normed_all, grad_k),
            contract_rows(normed_all, grad_v),
        ]
    )
    grad_normed = lax.psum_scatter(
        times_transposed(grad_q, qkv_w[0])
        + times_transposed(grad_k, qkv_w[1])
        + times_transposed(grad_v, qkv_w[2]),
        "tensor",
        scatter_dimension=0,
        tiled=True,
    )
    ln_one_gain_grad = jnp.sum(grad_normed * normal_one, axis=0)
    ln_one_bias_grad = jnp.sum(grad_normed, axis=0)
    grad_start = grad_middle + norm_back(grad_normed, normal_one, inverse_one, norm_gains[0])
    patch_grad = jnp.where(masked[:, None], 0.0, grad_start)
    token_grad = jnp.sum(jnp.where(masked[:, None], grad_start, 0.0), axis=0)
    qkv_owned, out_owned, up_owned, down_owned = (
        lax.psum_scatter(qkv_grad, "dp", scatter_dimension=1, tiled=True),
        lax.psum_scatter(grad_outw, "dp", scatter_dimension=1, tiled=True),
        lax.psum_scatter(up_grad, "dp", scatter_dimension=0, tiled=True),
        lax.psum_scatter(grad_down, "dp", scatter_dimension=1, tiled=True),
    )
    zero_row = jnp.zeros((width,), jnp.float32)
    query_bias_grad = lax.dynamic_update_slice_in_dim(
        zero_row, jnp.sum(grad_q.astype(jnp.float32), axis=0), tensor_id * lanes, 0
    )
    value_bias_grad = lax.dynamic_update_slice_in_dim(
        zero_row, jnp.sum(grad_v.astype(jnp.float32), axis=0), tensor_id * lanes, 0
    )
    up_bias_grad = lax.dynamic_update_slice_in_dim(
        jnp.zeros((FF,), jnp.float32), up_bias_part, tensor_id * hidden_lanes, 0
    ).reshape(-1, width)
    gain_grad = jnp.stack([ln_one_gain_grad, ln_two_gain_grad, scale_one_grad, scale_two_grad])
    shift_grad = jnp.concatenate(
        [
            jnp.stack(
                [
                    ln_one_bias_grad,
                    query_bias_grad,
                    value_bias_grad,
                    out_bias_grad,
                    ln_two_bias_grad,
                    down_bias_grad,
                    token_grad,
                ]
            ),
            up_bias_grad,
        ],
        axis=0,
    )
    gain_total, shift_total = lax.psum((gain_grad, shift_grad), ("dp", "tensor"))
    correction = 1.0 - jnp.power(jnp.float32(0.5), step_count[0].astype(jnp.float32))
    qkv_res = adamw_step(
        qkv_master, qkv_first, qkv_second, qkv_owned, D ** (-0.5), DECAY, correction
    )
    out_res = adamw_step(
        out_master, out_first, out_second, out_owned, (D // 16) ** (-0.5), DECAY, correction
    )
    up_res = adamw_step(up_master, up_first, up_second, up_owned, D ** (-0.5), DECAY, correction)
    down_res = adamw_step(
        down_master, down_first, down_second, down_owned, FF ** (-0.5), DECAY, correction
    )
    gain_res = adamw_step(norm_gains, gain_first, gain_second, gain_total, 0.1, 0.0, correction)
    shift_res = adamw_step(shifts, shift_first, shift_second, shift_total, 0.3, 0.0, correction)
    return (
        layer_out,
        patch_grad,
        qkv_res[0],
        qkv_res[1],
        qkv_res[2],
        qkv_res[3],
        out_res[0],
        out_res[1],
        out_res[2],
        out_res[3],
        up_res[0],
        up_res[1],
        up_res[2],
        up_res[3],
        down_res[0],
        down_res[1],
        down_res[2],
        down_res[3],
        gain_res[0],
        gain_res[1],
        gain_res[2],
        gain_res[3],
        shift_res[0],
        shift_res[1],
        shift_res[2],
        shift_res[3],
    )


def solution(mesh):
    placed = (
        P(("dp", "tensor"), None),
        P(("dp", "tensor"), None),
        P(("dp", "tensor")),
        P("dp"),
        P(),
        P(),
        P(),
        P(None, "dp", "tensor"),
        P(None, "dp", "tensor"),
        P(None, "dp", "tensor"),
        P("tensor", "dp"),
        P("tensor", "dp"),
        P("tensor", "dp"),
        P("dp", "tensor"),
        P("dp", "tensor"),
        P("dp", "tensor"),
        P("tensor", "dp"),
        P("tensor", "dp"),
        P("tensor", "dp"),
        P(),
        P(),
        P(),
        P(),
        P(),
        P(),
    )
    return jax.shard_map(
        on_device,
        mesh=mesh,
        in_specs=placed,
        out_specs=(
            P(("dp", "tensor"), None),
            P(("dp", "tensor"), None),
            P(None, "dp", "tensor"),
            P(None, "dp", "tensor"),
            P(None, "dp", "tensor"),
            P(None, "dp", "tensor"),
            P("tensor", "dp"),
            P("tensor", "dp"),
            P("tensor", "dp"),
            P("tensor", "dp"),
            P("dp", "tensor"),
            P("dp", "tensor"),
            P("dp", "tensor"),
            P("dp", "tensor"),
            P("tensor", "dp"),
            P("tensor", "dp"),
            P("tensor", "dp"),
            P("tensor", "dp"),
            P(),
            P(),
            P(),
            P(),
            P(),
            P(),
            P(),
            P(),
        ),
        check_vma=False,
    )
```

profile of v0, /device:TPU:0, one launch (start us, length us, event | category | flops | bytes accessed | tf_op | source)
XLA Modules:
  0.0 834.1 jit_solution(14950640881732094366)
XLA Ops:
  17.3 33.0 %all_gather.30 = bf16[192,768]{0,1:T(8,128)(2,1)S(1)} all-gather(bf16[192,96]{0,1:T(8,128)(2,1)S(1)} %copy.70), channel_id=1, replica_groups=mesh['dp'=8,'tensor'=4] {'dp'}, dimensions={1}, use_global_device_ids=true | all-gather | bytes 331776 | tf_op jit(solution)/shard_map/all_gather | solution.py:253
  50.2 34.6 %all_gather.29 = bf16[3,768,192]{2,1,0:T(8,128)(2,1)S(1)} all-gather(bf16[3,96,192]{2,1,0:T(8,128)(2,1)} %convert_element_type.155), channel_id=1, replica_groups=mesh['dp'=8,'tensor'=4] {'dp'}, dimensions={1}, use_global_device_ids=true | all-gather | bytes 995328 | tf_op jit(solution)/shard_map/all_gather | solution.py:252
  85.9 3.4 fusion.19
  89.4 2.2 convolution_convert_fusion.2
  92.6 3.1 fusion.20
  96.6 39.9 %while.26 = (s32[]{:T(128)}, bf16[4,512,192]{1,2,0:T(8,128)(2,1)}, f32[4,3,512]{2,1,0:T(4,128)S(1)}, s32[4]{0:T(128)S(1)}, bf16[2560,192]{0,1:T(8,128)(2,1)S(1)}...) while((s32[]{:T(128)}, bf16[4,512,192]{1,2,0:T(8,128)(2,1)}, ...), condition=%wide.region_5.6_spmd, body=%wide.region_2.5_spmd.sunk | while | flops 422148608 | bytes 24584440 | solution.py:114
  103.6 2.3 fusion.132
  113.6 2.3 fusion.132
  123.5 2.3 fusion.132
  133.5 2.2 fusion.132
  139.0 3.7 fusion.63
  144.4 57.4 %reduce-scatter.13.cloned.1.call-done = f32[512,768]{1,0:T(8,128)} async-done(((f32[2048,768]{1,0:T(8,128)}), f32[512,768]{1,0:T(8,128)}) %reduce-scatter.13.cloned.1.call-update) | async-done | bytes 1572880 | tf_op jit(solution)/shard_map/reduce_scatter | solution.py:286
  209.3 24.5 %all-gather.9.cloned.1.call-done = bf16[2048,768]{1,0:T(8,128)(2,1)} async-done(((bf16[512,768]{1,0:T(8,128)(2,1)}), bf16[2048,768]{1,0:T(8,128)(2,1)}) %all-gather.9.cloned.1.call-update) | async-done | bytes 3145744 | tf_op jit(solution)/shard_map/all_gather | solution.py:296
  233.7 7.5 fusion.64
  241.2 36.9 %all-gather.13.cloned.1.call-done = bf16[768,768]{0,1:T(8,128)(2,1)} async-done(((bf16[768,96]{0,1:T(8,128)(2,1)}), bf16[768,768]{0,1:T(8,128)(2,1)}) %all-gather.13.cloned.1.call-update) | async-done | bytes 1179664 | tf_op jit(solution)/shard_map/all_gather | solution.py:255
  278.1 29.1 %all-gather.15.cloned.1.call-done = bf16[2048,768]{1,0:T(8,128)(2,1)} async-done(((bf16[512,768]{1,0:T(8,128)(2,1)}), bf16[2048,768]{1,0:T(8,128)(2,1)}) %all-gather.15.cloned.1.call-update) | async-done | bytes 3145744 | tf_op jit(solution)/shard_map/all_gather | solution.py:320
  307.3 20.5 %convert_reduce_fusion = (f32[768]{0:T(1024)}, bf16[2048,768]{1,0:T(8,128)(2,1)S(1)}, f32[2048,768]{1,0:T(8,128)}) fusion(f32[2048,768]{1,0:T(8,128)} %fusion.64, f32[768]{0:T(1024)S(1)} %dynamic_slice.76, bf16[2048,768]{1,0:T(8,128)(2,1)} %all-gather.15.cloned.1.call-done, bf16[768,768]{0,1:T(8,128)(2,1)} %all-gather.13.cloned.1.call-done), kind=kOutput, calls=%fused_computation.39 | convolution fusion | flops 2533883136 | bytes 20060160 | tf_op jit(solution)/shard_map/dot_general | solution.py:43
  329.5 4.5 fusion.65
  334.1 5.6 multiply_convert_fusion.1
  341.4 4.0 convolution_convert_fusion
  345.5 46.9 %reduce-scatter.17.cloned.1.call-done = f32[512,768]{1,0:T(8,128)} async-done(((f32[2048,768]{1,0:T(8,128)}), f32[512,768]{1,0:T(8,128)}) %reduce-scatter.17.cloned.1.call-update) | async-done | bytes 1572880 | tf_op jit(solution)/shard_map/reduce_scatter | solution.py:327
  392.4 2.9 multiply_reduce_fusion.3
  395.3 37.5 %reduce-scatter.15.cloned.1.call-done = bf16[512,768]{1,0:T(8,128)(2,1)} async-done(((bf16[2048,768]{1,0:T(8,128)(2,1)}), bf16[512,768]{1,0:T(8,128)(2,1)}) %reduce-scatter.15.cloned.1.call-update) | async-done | bytes 786448 | tf_op jit(solution)/shard_map/reduce_scatter | solution.py:301
  432.8 4.1 convert_reduce_fusion.2
  437.2 6.9 fusion.66
  444.2 7.6 fusion.67
  451.8 13.8 %all-gather.17.cloned.1.call-done = bf16[2048,768]{1,0:T(8,128)(2,1)} async-done(((bf16[512,768]{1,0:T(8,128)(2,1)}), bf16[2048,768]{1,0:T(8,128)(2,1)}) %all-gather.17.cloned.1.call-update) | async-done | bytes 3145744 | tf_op jit(solution)/shard_map/all_gather | solution.py:336
  465.6 4.2 convolution_bitcast_fusion
  470.0 4.0 convolution_convert_fusion.1
  475.8 77.3 %while.27 = (s32[]{:T(128)}, f32[2560,192]{0,1:T(8,128)S(1)}, f32[2560,192]{0,1:T(8,128)}, bf16[4,512,192]{1,2,0:T(8,128)(2,1)S(1)}, s32[4]{0:T(128)S(1)}, /*ind...) while((s32[]{:T(128)}, f32[2560,192]{0,1:T(8,128)S(1)}, ...), condition=%wide.region_15.16_spmd, body=%wide.region_13.15_spmd.sunk | while | flops 1031535104 | bytes 76280184 | solution.py:192
  484.7 1.9 fusion.144
  486.6 2.5 multiply_reduce_fusion.12
  505.9 2.5 multiply_reduce_fusion.12
  523.2 1.9 fusion.144
  525.1 2.5 multiply_reduce_fusion.12
  544.4 2.5 multiply_reduce_fusion.12
  555.5 2.7 convolution_bitcast_fusion.3
  562.0 4.2 copy.80
  566.2 4.7 reshape.257
  571.3 2.2 fusion.24
  575.0 3.8 add_add_fusion
  584.1 2.1 fusion.53
  586.2 2.2 fusion.51
  594.9 55.4 %reduce-scatter.27.cloned.1.call-done = f32[96,192]{1,0:T(8,128)} async-done(((f32[768,192]{1,0:T(8,128)}), f32[96,192]{1,0:T(8,128)}) %reduce-scatter.27.cloned.1.call-update) | async-done | bytes 73744
  653.1 66.8 %reduce-scatter.25.cloned.1.call-done = f32[96,576]{1,0:T(8,128)} async-done(((f32[768,576]{1,0:T(8,128)}), f32[96,576]{1,0:T(8,128)}) %reduce-scatter.25.cloned.1.call-update) | async-done | bytes 221200
  728.7 51.0 %reduce-scatter.19.cloned.1.call-done = f32[512,768]{1,0:T(8,128)} async-done(((f32[2048,768]{1,0:T(8,128)}), f32[512,768]{1,0:T(8,128)}) %reduce-scatter.19.cloned.1.call-update) | async-done | bytes 1572880 | tf_op jit(solution)/shard_map/reduce_scatter | solution.py:349
  779.7 2.3 multiply_reduce_fusion.4
  785.0 40.0 %all-reduce.3 = (f32[4,768]{1,0:T(4,128)S(1)}, f32[11,768]{1,0:T(8,128)S(1)}) all-reduce(f32[4,768]{1,0:T(4,128)S(1)} %pad_maximum_fusion.1, f32[11,768]{1,0:T(8,128)S(1)} %concatenate.3), channel_id=1, replica_groups=mesh['dp'=8,'tensor'=4] {'dp','tensor'}, use_global_device_ids=true, to_apply=%region_27.28 | all-reduce | flops 11520 | bytes 92160 | tf_op jit(solution)/shard_map/psum | solution.py:396
  (373 shorter events, 143.9 us)
Async XLA Ops:
  8.1 76.8 %all-gather.7.cloned.1.call-start = ((), (), s32[]{:S(2)}) async-start(), calls=%async_computation.8 | async-start | bytes 3932160 | tf_op jit(solution)/shard_map/all_gather | solution.py:276
  11.5 190.4 %copy-start.48 = (f32[768]{0:T(1024)}, f32[768]{0:T(1024)S(1)}, u32[]{:S(2)}) copy-start(f32[768]{0:T(1024)S(1)} %get-tuple-element.335) | copy-start | bytes 9220
  14.7 187.2 %copy-start.2 = (f32[512,768]{1,0:T(8,128)}, f32[512,768]{1,0:T(8,128)S(1)}, u32[]{:S(2)}) copy-start(f32[512,768]{1,0:T(8,128)S(1)} %get-tuple-element.341) | copy-start | bytes 4718596
  16.3 185.6 %reduce-scatter.13.cloned.1.call-start = ((), (), s32[]{:S(2)}) async-start(), calls=%async_computation.9 | async-start | bytes 7864320 | tf_op jit(solution)/shard_map/reduce_scatter | solution.py:286
  50.2 87.8 %copy-start.21 = (bf16[192,768]{0,1:T(8,128)(2,1)}, bf16[192,768]{0,1:T(8,128)(2,1)S(1)}, u32[]{:S(2)}) copy-start(bf16[192,768]{0,1:T(8,128)(2,1)S(1)} %all_gather.30) | copy-start | bytes 884740
  136.5 6.2 copy-start.10
  142.8 66.5 %all-gather.11.cloned.1.call-start = ((), (), s32[]{:S(2)}) async-start(), calls=%async_computation.11 | async-start | bytes 1327104 | tf_op jit(solution)/shard_map/all_gather | solution.py:254
  144.4 89.3 %all-gather.9.cloned.1.call-start = ((), (), s32[]{:S(2)}) async-start(), calls=%async_computation.10 | async-start | bytes 3932160 | tf_op jit(solution)/shard_map/all_gather | solution.py:296
  205.2 72.9 %all-gather.13.cloned.1.call-start = ((), (), s32[]{:S(2)}) async-start(), calls=%async_computation.12 | async-start | bytes 1327104 | tf_op jit(solution)/shard_map/all_gather | solution.py:255
  206.0 101.3 %all-gather.15.cloned.1.call-start = ((), (), s32[]{:S(2)}) async-start(), calls=%async_computation.14 | async-start | bytes 3932160 | tf_op jit(solution)/shard_map/all_gather | solution.py:320
  207.8 184.5 %reduce-scatter.17.cloned.1.call-start = ((), (), s32[]{:S(2)}) async-start(), calls=%async_computation.15 | async-start | bytes 7864320 | tf_op jit(solution)/shard_map/reduce_scatter | solution.py:327
  241.2 88.3 %copy-start.68 = (bf16[768,768]{1,0:T(8,128)(2,1)S(1)}, bf16[768,768]{1,0:T(8,128)(2,1)}, u32[]{:S(2)}) copy-start(bf16[768,768]{1,0:T(8,128)(2,1)} %all-gather.11.cloned.1.call-done) | copy-start | bytes 3538948
  334.1 98.7 %reduce-scatter.15.cloned.1.call-start = ((), (), s32[]{:S(2)}) async-start(), calls=%async_computation.13 | async-start | bytes 3932160 | tf_op jit(solution)/shard_map/reduce_scatter | solution.py:301
  334.1 7.3 copy-start.69
  345.4 87.4 %copy-start.53 = (f32[768]{0:T(1024)S(1)}, f32[768]{0:T(1024)}, u32[]{:S(2)}) copy-start(f32[768]{0:T(1024)} %get-tuple-element.337) | copy-start | bytes 9220
  345.5 120.2 %all-gather.17.cloned.1.call-start = ((), (), s32[]{:S(2)}) async-start(), calls=%async_computation.16 | async-start | bytes 3932160 | tf_op jit(solution)/shard_map/all_gather | solution.py:336
  392.4 40.4 %copy-start.16 = (f32[512,768]{1,0:T(8,128)S(1)}, f32[512,768]{1,0:T(8,128)}, u32[]{:S(2)}) copy-start(f32[512,768]{1,0:T(8,128)} %reduce-scatter.17.cloned.1.call-done) | copy-start | bytes 4718596
  436.9 147.2 %reduce-scatter.21.cloned.1.call-start = ((), (), s32[]{:S(2)}) async-start(), calls=%async_computation.18 | async-start | bytes 2654208 | tf_op jit(solution)/shard_map/reduce_scatter | solution.py:365
  444.1 21.5 %copy-start.20 = (bf16[4,24,8,512]{3,2,0,1:T(8,128)(2,1)S(1)}, bf16[4,24,8,512]{3,2,0,1:T(8,128)(2,1)}, u32[]{:S(2)}) copy-start(bf16[4,24,8,512]{3,2,0,1:T(8,128)(2,1)} %copy-done.19) | copy-start | bytes 2359300
  444.1 142.1 %reduce-scatter.23.cloned.1.call-start = ((), (), s32[]{:S(2)}) async-start(), calls=%async_computation.19 | async-start | bytes 2654208 | tf_op jit(solution)/shard_map/reduce_scatter | solution.py:366
  451.8 198.5 %reduce-scatter.27.cloned.1.call-start = ((), (), s32[]{:S(2)}) async-start(), calls=%async_computation.21 | async-start | bytes 884736
  451.8 18.1 %copy-start.22 = (bf16[192,768]{0,1:T(8,128)(2,1)S(1)}, bf16[192,768]{0,1:T(8,128)(2,1)}, u32[]{:S(2)}) copy-start(bf16[192,768]{0,1:T(8,128)(2,1)} %copy-done.21) | copy-start | bytes 884740
  469.9 250.0 %reduce-scatter.25.cloned.1.call-start = ((), (), s32[]{:S(2)}) async-start(), calls=%async_computation.20 | async-start | bytes 2211840
  570.9 208.7 %reduce-scatter.19.cloned.1.call-start = ((), (), s32[]{:S(2)}) async-start(), calls=%async_computation.17 | async-start | bytes 7864320 | tf_op jit(solution)/shard_map/reduce_scatter | solution.py:349
  578.7 5.4 copy-start.26
  578.8 5.4 copy-start.33
  579.7 6.5 copy-start.28
  579.7 13.1 %copy-start.12 = (bf16[4,512,192]{1,2,0:T(8,128)(2,1)S(1)}, bf16[4,512,192]{1,2,0:T(8,128)(2,1)}, u32[]{:S(2)}) copy-start(bf16[4,512,192]{1,2,0:T(8,128)(2,1)} %copy-done.11) | copy-start | bytes 2359300
  579.9 6.4 copy-start.35
  582.6 68.7 %copy-start.32 = (f32[192,96]{1,0:T(8,128)S(1)}, f32[192,96]{1,0:T(8,128)}, u32[]{:S(2)}) copy-start(f32[192,96]{1,0:T(8,128)} %param.39) | copy-start | bytes 221188
  582.6 68.7 %copy-start.38 = (f32[192,96]{1,0:T(8,128)S(1)}, f32[192,96]{1,0:T(8,128)}, u32[]{:S(2)}) copy-start(f32[192,96]{1,0:T(8,128)} %param.41) | copy-start | bytes 221188
  594.9 55.4 %copy-start.62 = (f32[1,768]{1,0:T(1,128)}, f32[1,768]{1,0:T(1,128)S(1)}, u32[]{:S(2)}) copy-start(f32[1,768]{1,0:T(1,128)S(1)} %dynamic_update_slice.29) | copy-start | bytes 9220
  651.3 128.4 %copy-start.3 = (f32[512,768]{1,0:T(8,128)S(1)}, f32[512,768]{1,0:T(8,128)}, u32[]{:S(2)}) copy-start(f32[512,768]{1,0:T(8,128)} %copy-done.2) | copy-start | bytes 4718596
  651.3 128.3 %copy-start.40 = (f32[768]{0:T(1024)S(1)}, f32[768]{0:T(1024)}, u32[]{:S(2)}) copy-start(f32[768]{0:T(1024)} %copy-done.39) | copy-start | bytes 9220
  651.3 128.3 %copy-start.42 = (f32[512]{0:T(512)S(1)}, f32[512]{0:T(512)}, u32[]{:S(2)}) copy-start(f32[512]{0:T(512)} %copy-done.41) | copy-start | bytes 6148
  651.4 128.3 %copy-start.51 = (f32[512]{0:T(512)S(1)}, f32[512]{0:T(512)}, u32[]{:S(2)}) copy-start(f32[512]{0:T(512)} %copy-done.50) | copy-start | bytes 6148
  722.2 59.8 %copy-start.17 = (f32[512,768]{1,0:T(8,128)S(1)}, f32[512,768]{1,0:T(8,128)}, u32[]{:S(2)}) copy-start(f32[512,768]{1,0:T(8,128)} %reduce-scatter.13.cloned.1.call-done) | copy-start | bytes 4718596
  722.3 59.8 %copy-start.43 = (f32[512]{0:T(512)S(1)}, f32[512]{0:T(512)}, u32[]{:S(2)}) copy-start(f32[512]{0:T(512)} %copy-done.41) | copy-start | bytes 6148
  722.3 59.8 %copy-start.49 = (f32[768]{0:T(1024)S(1)}, f32[768]{0:T(1024)}, u32[]{:S(2)}) copy-start(f32[768]{0:T(1024)} %copy-done.48) | copy-start | bytes 9220
  722.3 59.8 %copy-start.52 = (f32[512]{0:T(512)S(1)}, f32[512]{0:T(512)}, u32[]{:S(2)}) copy-start(f32[512]{0:T(512)} %copy-done.50) | copy-start | bytes 6148
  722.3 59.8 %copy-start.67 = (pred[512]{0:T(512)(128)(4,1)S(1)}, pred[512]{0:T(512)(128)(4,1)}, u32[]{:S(2)}) copy-start(pred[512]{0:T(512)(128)(4,1)} %copy-done.66) | copy-start | bytes 1540
  782.1 44.2 %copy-start.1 = (bf16[197,768]{1,0:T(8,128)(2,1)S(1)}, bf16[197,768]{1,0:T(8,128)(2,1)}, u32[]{:S(2)}) copy-start(bf16[197,768]{1,0:T(8,128)(2,1)} %param.33) | copy-start | bytes 907780
  783.3 41.7 %copy-start.44 = (f32[4,768]{1,0:T(4,128)S(1)}, f32[4,768]{1,0:T(4,128)}, u32[]{:S(2)}) copy-start(f32[4,768]{1,0:T(4,128)} %param.48) | copy-start | bytes 36868
  783.3 41.7 %copy-start.57 = (f32[4,768]{1,0:T(4,128)S(1)}, f32[4,768]{1,0:T(4,128)}, u32[]{:S(2)}) copy-start(f32[4,768]{1,0:T(4,128)} %param.50) | copy-start | bytes 36868
  783.3 41.7 %copy-start.58 = (f32[4,768]{1,0:T(4,128)S(1)}, f32[4,768]{1,0:T(4,128)}, u32[]{:S(2)}) copy-start(f32[4,768]{1,0:T(4,128)} %param.49) | copy-start | bytes 36868
  783.3 42.3 %copy-start.37 = (f32[11,768]{1,0:T(8,128)S(1)}, f32[11,768]{1,0:T(8,128)}, u32[]{:S(2)}) copy-start(f32[11,768]{1,0:T(8,128)} %param.51) | copy-start | bytes 101380
  783.3 42.3 %copy-start.46 = (f32[11,768]{1,0:T(8,128)S(1)}, f32[11,768]{1,0:T(8,128)}, u32[]{:S(2)}) copy-start(f32[11,768]{1,0:T(8,128)} %param.53) | copy-start | bytes 101380
  783.3 42.3 %copy-start.47 = (f32[11,768]{1,0:T(8,128)S(1)}, f32[11,768]{1,0:T(8,128)}, u32[]{:S(2)}) copy-start(f32[11,768]{1,0:T(8,128)} %param.52) | copy-start | bytes 101380
  (43 other events, 88.1 us)
Sparse Core Ops, SparseCore 0:
  16.4 31.2 all-gather.6
  142.9 58.9 reduce-scatter.12
  437.1 28.5 all-gather.16
Sparse Core Ops, SparseCore 1:
  146.0 42.1 all-gather.10
  205.3 28.4 all-gather.8
  236.6 41.5 all-gather.12
  280.4 26.8 all-gather.14
  334.1 58.2 reduce-scatter.16
  394.9 37.8 reduce-scatter.14
  444.2 69.0 reduce-scatter.20
  517.0 68.1 reduce-scatter.22
  588.7 61.6 reduce-scatter.26
  653.8 66.0 reduce-scatter.24
  722.5 57.2 reduce-scatter.18
where the time goes:
time: 845 us; the launch traced here: 834 us
  waiting for transfers between devices  420 us (50%)
  matrix products  129 us (15%)
  blocking collectives  108 us (13%)
  local copies, waits for them, and re-layouts  87.4 us (10%)
  other arithmetic  57.4 us (7%)
  between operations  18.5 us (2%)
  loops' own time  13.7 us (2%)
    unnamed x16, waiting for transfers between devices  122 us
    reduce_scatter x1, waiting for transfers between devices, on_device(): lax.psum_scatter(jnp.dot(mixed_all, out_w, preferred_element_type=jnp.flo...  57.4 us
    reduce_scatter x1, waiting for transfers between devices, on_device(): lax.psum_scatter(times_transposed(grad_q, qkv_w[0]) + times_transposed(gr...  51 us
    reduce_scatter x1, waiting for transfers between devices, on_device(): lax.psum_scatter(times_transposed(pre_grad, up_w), 'tensor', scatter_dime...  46.9 us
    psum x1, blocking collectives, on_device(): lax.psum((gain_grad, shift_grad), ('dp', 'tensor'))  40 us
    reduce_scatter x1, waiting for transfers between devices, on_device(): lax.psum_scatter(jnp.dot(hidden_all, down_w, preferred_element_type=jnp.f...  37.5 us
    all_gather x1, waiting for transfers between devices, on_device(): lax.all_gather(down_master.astype(jnp.bfloat16), 'dp', axis=1, tiled=True)  36.9 us
    dot_general x6, matrix products, times_transposed(): lax.dot_general(left_rows, matrix, (((1,), (1,)), ((), ())), preferred_el...  36 us
  transfers between devices with their start and end apart: 14, of which 10 were waited for; matrix products, arithmetic and copies ran while one was open for 19% of the time, Pallas kernels for 0%

commit v1 on v0

v1 whole, which is shorter than its diff:
```python
import functools

import jax
import jax.numpy as jnp
from jax import lax
from jax.experimental import pallas as pl
from jax.experimental.pallas import tpu as pltpu
from jax.sharding import PartitionSpec as P

D = 768
HEAD_DIM = 64
FF = 3072
BIG_LEN = 197
SMALL_LEN = 101
HALO = 208
ALIGN = 16
BIG_Q, BIG_K = 224, 256
SMALL_W = 128

EPS_NORM = 1e-06
ADAM_EPS = 1e-08
DECAY = 0.05
NEGATIVE = -1e30
FACTOR = HEAD_DIM ** (-0.5)
BF = jnp.bfloat16
F32 = jnp.float32


def send_dp(value, target):
    count = lax.axis_size("dp")
    return lax.ppermute(value, "dp", [(i, target(i)) for i in range(count)])


def send_x(value):
    return send_dp(value, lambda i: i ^ 1)


def send_tensor(value, mask):
    return lax.ppermute(value, "tensor", [(i, i ^ mask) for i in range(4)])


def send_y(value):
    return send_tensor(value, 2)


def send_core(value):
    return send_tensor(value, 1)


def z_digits():
    left = lax.axis_size("dp") // 2
    stride, digits = 1, []
    while left > 1:
        radix = 4 if left % 4 == 0 else 2
        digits.append((stride, radix))
        stride, left = stride * radix, left // radix
    return digits


def send_digit(value, stride, radix, step):
    def target(i):
        z, x = i // 2, i % 2
        digit = z // stride % radix
        return 2 * (z + ((digit + step) % radix - digit) * stride) + x

    return send_dp(value, target)


def gather_z(block):
    z = lax.axis_index("dp") // 2
    block = block[None]
    for stride, radix in z_digits():
        digit = z // stride % radix
        out = jnp.zeros((radix,) + block.shape, block.dtype)
        out = lax.dynamic_update_slice(out, block[None], (digit, 0, 0, 0))
        pieces = [send_digit(block, stride, radix, step) for step in range(1, radix)]
        for step, piece in enumerate(pieces, 1):
            out = lax.dynamic_update_slice(
                out, piece[None], ((digit + radix - step) % radix, 0, 0, 0)
            )
        block = out.reshape((-1,) + block.shape[1:])
    return block


def scatter_z(partial):
    z = lax.axis_index("dp") // 2
    for stride, radix in reversed(z_digits()):
        digit = z // stride % radix
        parts = partial.reshape((radix, -1) + partial.shape[1:])
        own = lax.dynamic_index_in_dim(parts, digit, 0, keepdims=False)
        pieces = [
            send_digit(
                lax.dynamic_index_in_dim(
                    parts, (digit + step) % radix, 0, keepdims=False
                ).astype(BF),
                stride,
                radix,
                step,
            )
            for step in range(1, radix)
        ]
        for piece in pieces:
            own = own + piece.astype(F32)
        partial = own
    return partial[0]


def interleave(mine, other):
    x = lax.axis_index("dp") % 2
    low = jnp.where(x == 0, mine, other)
    high = jnp.where(x == 0, other, mine)
    return jnp.stack([low, high], axis=1).reshape(-1, mine.shape[-1])


def gather_chunk(z_all):
    half = z_all.shape[-1] // 2
    from_x = send_x(z_all)
    from_y = send_y(z_all[..., half:])
    from_xy = send_x(from_y)
    own = interleave(z_all, from_x)
    across = send_y(own[:, :half])
    own_core = send_core(own)
    across = jnp.concatenate([across, interleave(from_y, from_xy)], axis=1)
    return own, own_core, across, send_core(across)


def scatter_chunk(own, across):
    count, n = lax.axis_size("dp"), own.shape[-1]
    half = n // 2
    x = lax.axis_index("dp") % 2

    def at_x(value, which):
        return lax.dynamic_index_in_dim(value, which, 1, keepdims=False)

    own = own.reshape(count // 2, 2, -1, n)
    across = across.reshape(count // 2, 2, -1, n)
    over_y = send_y(across[..., :half].astype(BF))
    far = jnp.stack([at_x(own[..., half:], 1 - x), at_x(across[..., half:], 1 - x)])
    over_x = send_x(far.astype(BF))
    low = own[..., :half] + over_y.astype(F32)
    high_across = at_x(across[..., half:], x) + over_x[1].astype(F32)
    low_x = send_x(at_x(low, 1 - x).astype(BF))
    high_y = send_y(high_across.astype(BF))
    low = at_x(low, x) + low_x.astype(F32)
    high = at_x(own[..., half:], x) + over_x[0].astype(F32) + high_y.astype(F32)
    return scatter_z(jnp.concatenate([low, high], axis=-1))


def sum_everywhere(value):
    value = value + send_core(value)
    across = send_y(value), send_x(value), send_x(send_y(value))
    value = (value + across[1]) + (across[0] + across[2])
    count = lax.axis_size("dp")
    bit = 2
    while bit < count:
        value = value + send_dp(value, lambda i, b=bit: i ^ b)
        bit *= 2
    return value


def image_loops(bounds, window_loop):
    big_rows, total = bounds[4], bounds[6]

    def big(index, carry):
        window_loop(index * BIG_LEN, index * BIG_LEN + BIG_LEN, BIG_Q, BIG_K)
        return carry

    def small(index, carry):
        start = big_rows + index * SMALL_LEN
        window_loop(start, jnp.minimum(start + SMALL_LEN, total), SMALL_W, SMALL_W)
        return carry

    lax.fori_loop(bounds[0], bounds[1], big, 0)
    lax.fori_loop(bounds[2], bounds[3], small, 0)


def image_bounds(count_big, first_row, local_rows, total_rows):
    big_rows = count_big * BIG_LEN
    last_row = first_row + local_rows - 1
    big_from = jnp.minimum(first_row // BIG_LEN, count_big)
    big_to = jnp.minimum(last_row // BIG_LEN + 1, count_big)
    small_from = jnp.maximum(first_row - big_rows, 0) // SMALL_LEN
    small_to = jnp.where(last_row >= big_rows, (last_row - big_rows) // SMALL_LEN + 1, small_from)
    base = first_row - HALO
    return jnp.stack(
        [big_from, big_to, small_from, small_to, big_rows, base, jnp.int32(total_rows), base]
    ).astype(jnp.int32)


def masks(start, stop, base, ext_rows, rows, keys):
    aligned = (start - base) // ALIGN * ALIGN
    at_q = pl.multiple_of(jnp.minimum(aligned, ext_rows - rows), ALIGN)
    at_k = pl.multiple_of(jnp.minimum(aligned, ext_rows - keys), ALIGN)

    def inside(offset, shape, axis):
        ids = lax.broadcasted_iota(jnp.int32, shape, axis) + (offset + base)
        return (ids >= start) & (ids < stop)

    return (
        at_q,
        at_k,
        inside(at_q, (rows, 1), 0),
        inside(at_k, (1, keys), 1),
        inside(at_k, (keys, 1), 0),
    )


def dot_nt(left, right):
    return lax.dot_general(left, right, (((1,), (1,)), ((), ())), preferred_element_type=F32)


def dot_tn(left, right):
    return lax.dot_general(left, right, (((0,), (0,)), ((), ())), preferred_element_type=F32)


def dot_nn(left, right):
    return jnp.dot(left, right, preferred_element_type=F32)


def attention_forward_kernel(bounds, *refs):
    qkv, outs = refs[:4], refs[4:]
    ext_rows = qkv[0].shape[0]

    def window(start, stop, rows, keys):
        at_q, at_k, row_in, key_in, _ = masks(start, stop, bounds[5], ext_rows, rows, keys)
        for source, out in zip(qkv, outs):
            width = out.shape[1]
            parts = []
            for at in range(0, width, HEAD_DIM):
                query = source[pl.ds(at_q, rows), at : at + HEAD_DIM]
                key = source[pl.ds(at_k, keys), width + at : width + at + HEAD_DIM]
                value = source[pl.ds(at_k, keys), 2 * width + at : 2 * width + at + HEAD_DIM]
                scores = jnp.where(key_in, dot_nt(query, key) * FACTOR, NEGATIVE)
                exps = jnp.exp(scores - jnp.max(scores, axis=-1, keepdims=True))
                probs = exps * (1.0 / jnp.sum(exps, axis=-1, keepdims=True))
                parts.append(dot_nn(probs.astype(BF), value))
            mixed = jnp.concatenate(parts, axis=1).astype(BF)
            old = out[pl.ds(at_q, rows), :]
            out[pl.ds(at_q, rows), :] = jnp.where(row_in, mixed, old)

    image_loops(bounds, window)


def attention_backward_kernel(bounds, *refs):
    qkv, grads, outs = refs[:4], refs[4:8], refs[8:]
    ext_rows = qkv[0].shape[0]

    def window(start, stop, rows, keys):
        at_q, at_k, row_in, key_in, key_row_in = masks(
            start, stop, bounds[5], ext_rows, rows, keys
        )
        both = row_in & key_in
        for source, grad, out in zip(qkv, grads, outs):
            width = grad.shape[1]
            query_parts, key_parts, value_parts = [], [], []
            for at in range(0, width, HEAD_DIM):
                query = source[pl.ds(at_q, rows), at : at + HEAD_DIM]
                key = source[pl.ds(at_k, keys), width + at : width + at + HEAD_DIM]
                value = source[pl.ds(at_k, keys), 2 * width + at : 2 * width + at + HEAD_DIM]
                grad_rows = grad[pl.ds(at_q, rows), at : at + HEAD_DIM]
                scores = jnp.where(key_in, dot_nt(query, key) * FACTOR, NEGATIVE)
                exps = jnp.exp(scores - jnp.max(scores, axis=-1, keepdims=True))
                probs = exps * (1.0 / jnp.sum(exps, axis=-1, keepdims=True))
                probs = jnp.where(both, probs, 0.0)
                weighted = probs * dot_nt(grad_rows, value)
                inner = jnp.sum(weighted, axis=-1, keepdims=True)
                grad_scores = (weighted - probs * inner).astype(BF)
                query_parts.append(dot_nn(grad_scores, key) * FACTOR)
                key_parts.append(dot_tn(grad_scores, query) * FACTOR)
                value_parts.append(dot_tn(probs.astype(BF), grad_rows))
            grad_query = jnp.concatenate(query_parts, axis=1).astype(BF)
            old = out[pl.ds(at_q, rows), :width]
            out[pl.ds(at_q, rows), :width] = jnp.where(row_in, grad_query, old)
            grad_kv = jnp.concatenate(key_parts + value_parts, axis=1).astype(BF)
            old = out[pl.ds(at_k, keys), width:]
            out[pl.ds(at_k, keys), width:] = jnp.where(key_row_in, grad_kv, old)

    image_loops(bounds, window)


def run_attention(kernel, name, bounds, inputs, out_width):
    ext_rows = inputs[0].shape[0]
    in_vmem = pl.BlockSpec(memory_space=pltpu.VMEM)
    return pl.pallas_call(
        kernel,
        name=name,
        in_specs=[pl.BlockSpec(memory_space=pltpu.SMEM)] + [in_vmem] * len(inputs),
        out_specs=[in_vmem] * 4,
        out_shape=[jax.ShapeDtypeStruct((ext_rows, out_width), BF)] * 4,
        compiler_params=pltpu.CompilerParams(vmem_limit_bytes=40 << 20),
    )(bounds, *inputs)


def exact_gelu(values):
    return jax.nn.gelu(values, approximate=False)


def norm_parts(values, gain, shift):
    average = jnp.mean(values, axis=-1, keepdims=True)
    centered = values - average
    inverse = lax.rsqrt(jnp.mean(centered * centered, axis=-1, keepdims=True) + EPS_NORM)
    normal_rows = centered * inverse
    return (normal_rows * gain + shift, normal_rows, inverse)


def norm_back(grad_rows, normal_rows, inverse, gain):
    scaled = grad_rows * gain
    return inverse * (
        scaled
        - jnp.mean(scaled, axis=-1, keepdims=True)
        - normal_rows * jnp.mean(scaled * normal_rows, axis=-1, keepdims=True)
    )


def adamw_step(master, first, second, gradient, rate, decay, correction):
    first_new = 0.5 * first + 0.5 * gradient
    second_new = 0.5 * second + 0.5 * gradient * gradient
    update = first_new / correction / (jnp.sqrt(second_new / correction) + ADAM_EPS)
    master_new = master - rate * (update + decay * master)
    return (master_new, first_new, second_new, master_new.astype(BF))


def to_absolute(parts):
    index = lax.axis_index("tensor")
    stacked = jnp.stack(parts).reshape(2, 2, -1)
    stacked = jnp.where(index // 2 == 1, stacked[::-1], stacked)
    return jnp.where(index % 2 == 1, stacked[:, ::-1], stacked).reshape(4, -1)


def on_device(
    patches,
    cotangent,
    mask_rows,
    count_big,
    pos_big,
    pos_small,
    step_count,
    qkv_master,
    qkv_first,
    qkv_second,
    out_master,
    out_first,
    out_second,
    up_master,
    up_first,
    up_second,
    down_master,
    down_first,
    down_second,
    norm_gains,
    gain_first,
    gain_second,
    shifts,
    shift_first,
    shift_second,
):
    tensor_id = lax.axis_index("tensor")
    local_rows = patches.shape[0]
    total_rows = 4 * local_rows
    lanes = qkv_master.shape[2]
    hidden_lanes = up_master.shape[1]
    big_rows = count_big[0] * BIG_LEN
    used_rows = big_rows + (total_rows - big_rows) // SMALL_LEN * SMALL_LEN
    first_row = tensor_id * local_rows

    payload = jnp.concatenate(
        [patches, jnp.broadcast_to(mask_rows[:, None].astype(BF), (local_rows, 128))], axis=1
    )
    up_hops, down_hops = [(0, 1), (1, 2), (2, 3)], [(1, 0), (2, 1), (3, 2)]
    before = lax.ppermute(payload[-HALO:], "tensor", up_hops)
    after = lax.ppermute(payload[:HALO], "tensor", down_hops)

    local_a = jnp.concatenate(
        [qkv_master[0], qkv_master[1], qkv_master[2], out_master.T], axis=1
    ).astype(BF)
    z_a = gather_z(local_a)
    local_b, local_c, z_a = lax.optimization_barrier(
        (up_master.astype(BF), down_master.astype(BF).T, z_a)
    )
    z_b = gather_z(local_b)
    a_all = gather_chunk(z_a)
    local_c, z_b = lax.optimization_barrier((local_c, z_b))
    z_c = gather_z(local_c)
    b_all = gather_chunk(z_b)
    c_all = gather_chunk(z_c)

    payload = jnp.concatenate([before, payload, after], axis=0)
    ext_rows = payload.shape[0]
    row_ids = first_row - HALO + jnp.arange(ext_rows, dtype=jnp.int32)
    remainder = row_ids - big_rows
    is_big = (row_ids >= 0) & (row_ids < big_rows)
    is_valid = (row_ids >= 0) & (row_ids < used_rows)
    is_small = is_valid & jnp.logical_not(is_big)
    position = jnp.where(is_big, row_ids % BIG_LEN, remainder % SMALL_LEN)
    masked_ext = (payload[:, D] == 1) & is_valid
    pick_big = (
        (position[:, None] == jnp.arange(BIG_LEN, dtype=jnp.int32)[None, :]) & is_big[:, None]
    ).astype(BF)
    pick_small = (
        (position[:, None] == jnp.arange(SMALL_LEN, dtype=jnp.int32)[None, :]) & is_small[:, None]
    ).astype(BF)
    placed = dot_nn(pick_big, pos_big) + dot_nn(pick_small, pos_small)
    start_ext = (
        jnp.where(masked_ext[:, None], shifts[6][None, :], payload[:, :D].astype(F32)) + placed
    )
    own = slice(HALO, HALO + local_rows)
    normed_ext, normal_ext, inverse_ext = norm_parts(start_ext, norm_gains[0], shifts[0])
    normed_ext = normed_ext.astype(BF)
    start_rows, masked, valid_local = start_ext[own], masked_ext[own], is_valid[own]
    normed, normal_one, inverse_one = normed_ext[own], normal_ext[own], inverse_ext[own]

    bounds = image_bounds(count_big[0], first_row, local_rows, total_rows)
    zero_bias = jnp.zeros((lanes,), F32)
    qkv_ext = []
    for step, weight in enumerate(a_all):
        at = (tensor_id ^ step) * lanes
        bias = jnp.concatenate(
            [
                lax.dynamic_slice_in_dim(shifts[1], at, lanes),
                zero_bias,
                lax.dynamic_slice_in_dim(shifts[2], at, lanes),
                zero_bias,
            ]
        )
        qkv_ext.append((dot_nn(normed_ext, weight) + bias).astype(BF))
    mixed = run_attention(attention_forward_kernel, "attention_forward", bounds, qkv_ext, lanes)
    mixed = [part[own] for part in mixed]
    out_w = [weight[:, 3 * lanes :] for weight in a_all]
    branch_attn = sum(dot_nt(part, weight) for part, weight in zip(mixed, out_w)) + shifts[3]
    middle = start_rows + norm_gains[2] * branch_attn
    normed_two, normal_two, inverse_two = norm_parts(middle, norm_gains[1], shifts[4])
    normed_two = normed_two.astype(BF)

    grad_out = cotangent.astype(F32) * valid_local[:, None].astype(F32)
    grad_branch = (norm_gains[3] * grad_out).astype(BF)
    up_bias = shifts[7:].reshape(-1)
    hidden, pre_grad = [], []
    for step in range(4):
        bias = lax.dynamic_slice_in_dim(up_bias, (tensor_id ^ step) * hidden_lanes, hidden_lanes)
        pre = dot_nn(normed_two, b_all[step]) + bias
        value, pull = jax.vjp(exact_gelu, pre)
        hidden.append(value.astype(BF))
        pre_grad.append(pull(dot_nn(grad_branch, c_all[step]))[0].astype(BF))

    def with_partner(rows, parts):
        sent = send_core(jnp.concatenate([rows, parts[1], parts[3]], axis=1))
        split = rows.shape[1], rows.shape[1] + parts[1].shape[1]
        other_rows = sent[:, : split[0]]
        return (
            dot_tn(rows, parts[0]) + dot_tn(other_rows, sent[:, split[0] : split[1]]),
            dot_tn(rows, parts[2]) + dot_tn(other_rows, sent[:, split[1] :]),
        )

    down_grad = scatter_chunk(*with_partner(grad_branch, hidden))
    grad_normed_two = sum(dot_nt(part, weight) for part, weight in zip(pre_grad, b_all))
    up_grad = scatter_chunk(*with_partner(normed_two, pre_grad))

    grad_middle = grad_out + norm_back(grad_normed_two, normal_two, inverse_two, norm_gains[1])
    grad_attn = (norm_gains[2] * grad_middle).astype(BF)
    before = lax.ppermute(grad_attn[-HALO:], "tensor", up_hops)
    after = lax.ppermute(grad_attn[:HALO], "tensor", down_hops)
    grad_attn_ext = jnp.concatenate([before, grad_attn, after], axis=0)
    grad_mixed = [dot_nn(grad_attn_ext, weight).astype(BF) for weight in out_w]
    grad_qkv = run_attention(
        attention_backward_kernel, "attention_backward", bounds, qkv_ext + grad_mixed, 3 * lanes
    )
    grad_qkv = [part[own] for part in grad_qkv]
    grad_normed = sum(
        dot_nt(part, weight[:, : 3 * lanes]) for part, weight in zip(grad_qkv, a_all)
    )
    qkv_pair = with_partner(normed, grad_qkv)
    out_pair = with_partner(grad_attn, mixed)
    a_grad = scatter_chunk(
        *(jnp.concatenate(pair, axis=1) for pair in zip(qkv_pair, out_pair))
    )

    branch_mlp = sum(dot_nt(part, weight) for part, weight in zip(hidden, c_all)) + shifts[5]
    layer_out = (middle + norm_gains[3] * branch_mlp).astype(BF)

    grad_start = grad_middle + norm_back(grad_normed, normal_one, inverse_one, norm_gains[0])
    patch_grad = jnp.where(masked[:, None], 0.0, grad_start)
    token_grad = jnp.sum(jnp.where(masked[:, None], grad_start, 0.0), axis=0)

    def column_sums(parts, at, width):
        return to_absolute([jnp.sum(part[:, at : at + width].astype(F32), axis=0) for part in parts])

    small = jnp.stack(
        [
            jnp.sum(grad_normed * normal_one, axis=0),
            jnp.sum(grad_normed_two * normal_two, axis=0),
            jnp.sum(grad_middle * branch_attn, axis=0),
            jnp.sum(grad_out * branch_mlp, axis=0),
            jnp.sum(grad_normed, axis=0),
            column_sums(grad_qkv, 0, lanes).reshape(-1),
            column_sums(grad_qkv, 2 * lanes, lanes).reshape(-1),
            jnp.sum(grad_attn.astype(F32), axis=0),
            jnp.sum(grad_normed_two, axis=0),
            jnp.sum(grad_branch.astype(F32), axis=0),
            token_grad,
        ]
    )
    small = jnp.concatenate([small, column_sums(pre_grad, 0, hidden_lanes)], axis=0)
    small = sum_everywhere(small)
    gain_total, shift_total = small[:4], small[4:]

    correction = 1.0 - jnp.power(jnp.float32(0.5), step_count[0].astype(F32))
    qkv_owned = jnp.stack([a_grad[:, i * lanes : (i + 1) * lanes] for i in range(3)])
    qkv_res = adamw_step(
        qkv_master, qkv_first, qkv_second, qkv_owned, D ** (-0.5), DECAY, correction
    )
    out_res = adamw_step(
        out_master, out_first, out_second, a_grad[:, 3 * lanes :].T, (D // 16) ** (-0.5), DECAY, correction
    )
    up_res = adamw_step(up_master, up_first, up_second, up_grad, D ** (-0.5), DECAY, correction)
    down_res = adamw_step(
        down_master, down_first, down_second, down_grad.T, FF ** (-0.5), DECAY, correction
    )
    gain_res = adamw_step(norm_gains, gain_first, gain_second, gain_total, 0.1, 0.0, correction)
    shift_res = adamw_step(shifts, shift_first, shift_second, shift_total, 0.3, 0.0, correction)
    return (
        (layer_out, patch_grad) + qkv_res + out_res + up_res + down_res + gain_res + shift_res
    )


def solution(mesh):
    rows = P(("dp", "tensor"), None)
    qkv = (P(None, "dp", "tensor"),)
    tensor_first, dp_first, whole = (P("tensor", "dp"),), (P("dp", "tensor"),), (P(),)
    weights = tuple(
        spec * 3 for spec in (qkv, tensor_first, dp_first, tensor_first)
    )
    results = tuple(
        spec * 4 for spec in (qkv, tensor_first, dp_first, tensor_first)
    )
    return jax.shard_map(
        on_device,
        mesh=mesh,
        in_specs=(rows, rows, P(("dp", "tensor")), P("dp")) + whole * 3 + sum(weights, ()) + whole * 6,
        out_specs=(rows, rows) + sum(results, ()) + whole * 8,
        check_vma=False,
    )
```

time: 845 us -> 458 us (0.54)
  waiting for transfers between devices: 420 us -> 103 us
  starting transfers between devices: 1.49 us -> 121 us
  blocking collectives: 108 us -> 0 us
  matrix products: 129 us -> 96.4 us
  Pallas kernels: 0 us -> 32.5 us
  local copies, waits for them, and re-layouts: 87.4 us -> 57.5 us
  other arithmetic: 57.4 us -> 38 us
  between operations: 18.5 us -> 4.4 us
  loops' own time: 13.7 us -> 0 us
    reduce_scatter x6 -> x0, waiting for transfers between devices: 193 us -> none  [the longest x1 57.4 us: on_device(): lax.psum_scatter(jnp.dot(mixed_all, out_w, preferred_element_type=jnp.flo...]
    unnamed x16 -> x0, waiting for transfers between devices: 122 us -> none
    ppermute x0 -> x62, starting transfers between devices: none -> 121 us  [the longest x34 60.3 us: send_dp(): return lax.ppermute(value, 'dp', [(i, target(i)) for i in range(count)])]
    all_gather x6 -> x0, waiting for transfers between devices: 104 us -> none  [the longest x1 36.9 us: on_device(): lax.all_gather(down_master.astype(jnp.bfloat16), 'dp', axis=1, tiled=True)]
    ppermute x0 -> x62, waiting for transfers between devices: none -> 103 us  [the longest x34 52.4 us: send_dp(): return lax.ppermute(value, 'dp', [(i, target(i)) for i in range(count)])]
    all_gather x2 -> x0, blocking collectives: 67.6 us -> none  [the longest x1 34.6 us: on_device(): lax.all_gather(qkv_master.astype(jnp.bfloat16), 'dp', axis=1, tiled=True)]
    psum x1 -> x0, blocking collectives: 40 us -> none  [on_device(): lax.psum((gain_grad, shift_grad), ('dp', 'tensor'))]
    pallas_call x0 -> x2, Pallas kernels: none -> 32.5 us  [run_attention(): pl.pallas_call(kernel, name=name, in_specs=[pl.BlockSpec(memory_space=plt...]
  transfers between devices with their start and end apart: 14 -> 62, of which waited for: 10 -> 22; matrix products, arithmetic and copies ran while one was open for 19% -> 29% of each run, Pallas kernels for 0% -> 2%
where the time goes in v1:
time: 458 us; the launch traced here: 452 us
  starting transfers between devices  121 us (26%)
  waiting for transfers between devices  103 us (22%)
  matrix products  96.4 us (21%)
  local copies, waits for them, and re-layouts  57.5 us (13%)
  other arithmetic  38 us (8%)
  Pallas kernels  32.5 us (7%)
    ppermute x34, starting transfers between devices, send_dp(): return lax.ppermute(value, 'dp', [(i, target(i)) for i in range(count)])  60.3 us
    ppermute x34, waiting for transfers between devices, send_dp(): return lax.ppermute(value, 'dp', [(i, target(i)) for i in range(count)])  52.4 us
    ppermute x24, waiting for transfers between devices, send_tensor(): return lax.ppermute(value, 'tensor', [(i, i ^ mask) for i in range(4)])  50.7 us
    dot_general x18, matrix products, dot_nn(): return jnp.dot(left, right, preferred_element_type=F32)  45.6 us
    ppermute x24, starting transfers between devices, send_tensor(): return lax.ppermute(value, 'tensor', [(i, i ^ mask) for i in range(4)])  40.8 us
    pallas_call x2, Pallas kernels, run_attention(): pl.pallas_call(kernel, name=name, in_specs=[pl.BlockSpec(memory_space=plt...  32.5 us
    dot_general x16, matrix products, dot_tn(): lax.dot_general(left, right, (((0,), (0,)), ((), ())), preferred_element_...  32.3 us
    unnamed x188, local copies, waits for them, and re-layouts  23.9 us
  transfers between devices with their start and end apart: 62, of which 22 were waited for; matrix products, arithmetic and copies ran while one was open for 29% of the time, Pallas kernels for 2%

profile of v1, /device:TPU:0, one launch (start us, length us, event | category | flops | bytes accessed | tf_op | source)
XLA Modules:
  0.0 452.4 jit_solution(13869929742639276354)
XLA Ops:
  3.1 3.1 collective-permute-start.2
  6.2 2.6 collective-permute-start.3
  12.5 3.8 collective-permute-start
  28.4 7.5 %collective-permute-done.11 = bf16[1,96,768]{2,1,0:T(8,128)(2,1)S(1)} collective-permute-done((bf16[1,96,768]{2,1,0:T(8,128)(2,1)S(1)}, bf16[1,96,768]{2,1,0:T(8,128)(2,1)S(1)}, u32[]{:S(2)}, u32[]{:S(2)}) %collective-permute-start.11) | collective-permute-done | bytes 147488 | tf_op jit(solution)/shard_map/ppermute | solution.py:31
  36.0 5.5 %collective-permute-done.12 = bf16[1,96,768]{2,1,0:T(8,128)(2,1)S(1)} collective-permute-done((bf16[1,96,768]{2,1,0:T(8,128)(2,1)S(1)}, bf16[1,96,768]{2,1,0:T(8,128)(2,1)S(1)}, u32[]{:S(2)}, u32[]{:S(2)}) %collective-permute-start.12) | collective-permute-done | bytes 147488 | tf_op jit(solution)/shard_map/ppermute | solution.py:31
  59.1 5.6 %collective-permute-done.22 = bf16[4,96,384]{2,1,0:T(8,128)(2,1)S(1)} collective-permute-done((bf16[4,96,384]{2,1,0:T(8,128)(2,1)S(1)}, bf16[4,96,384]{2,1,0:T(8,128)(2,1)S(1)}, u32[]{:S(2)}, u32[]{:S(2)}) %collective-permute-start.22) | collective-permute-done | bytes 294944 | tf_op jit(solution)/shard_map/ppermute | solution.py:39
  68.9 21.7 %collective-permute-done.9 = bf16[4,96,384]{2,1,0:T(8,128)(2,1)S(1)} collective-permute-done((bf16[4,96,384]{2,1,0:T(8,128)(2,1)S(1)}, bf16[4,96,384]{2,1,0:T(8,128)(2,1)S(1)}, u32[]{:S(2)}, u32[]{:S(2)}) %collective-permute-start.9) | collective-permute-done | bytes 294944 | tf_op jit(solution)/shard_map/ppermute | solution.py:31
  93.6 2.5 collective-permute-done.23
  97.6 4.5 collective-permute-done.26
  102.3 4.7 %collective-permute-done.7 = bf16[768,384]{1,0:T(8,128)(2,1)S(1)} collective-permute-done((bf16[768,384]{1,0:T(8,128)(2,1)S(1)}, bf16[768,384]{1,0:T(8,128)(2,1)S(1)}, u32[]{:S(2)}, u32[]{:S(2)}) %collective-permute-start.7) | collective-permute-done | bytes 589856 | tf_op jit(solution)/shard_map/ppermute | solution.py:39
  110.5 9.1 %collective-permute-done.21 = bf16[768,384]{1,0:T(8,128)(2,1)S(1)} collective-permute-done((bf16[768,384]{1,0:T(8,128)(2,1)S(1)}, bf16[768,384]{1,0:T(8,128)(2,1)S(1)}, u32[]{:S(2)}, u32[]{:S(2)}) %collective-permute-start.21) | collective-permute-done | bytes 589856 | tf_op jit(solution)/shard_map/ppermute | solution.py:39
  120.7 11.1 %collective-permute-done.24 = bf16[768,384]{1,0:T(8,128)(2,1)S(1)} collective-permute-done((bf16[768,384]{1,0:T(8,128)(2,1)S(1)}, bf16[768,384]{1,0:T(8,128)(2,1)S(1)}, u32[]{:S(2)}, u32[]{:S(2)}) %collective-permute-start.24) | collective-permute-done | bytes 589856 | tf_op jit(solution)/shard_map/ppermute | solution.py:39
  136.2 9.1 %attention_forward.1 = (bf16[928,192]{1,0:T(8,128)(2,1)S(1)}, bf16[928,192]{1,0:T(8,128)(2,1)S(1)}, bf16[928,192]{1,0:T(8,128)(2,1)S(1)}, bf16[928,192]{1,0:T(8,128)(2,1)S(1)}) custom-call(s32[8]{0:T(128)S(1)} %stack.202.bounds, bf16[928,768]{1,0:T(8,128)(2,1)S(1)} %add_convert_fusion.3.refs_0_, bf16[928,768]{1,0:T(8,128)(2,1)S(1)} %add_convert_fusion.2.refs_1_, ...), custom_call_target="tpu_custom_call" | custom-call | tf_op jit(solution)/shard_map/attention_forward/pallas_call | solution.py:284
  151.0 4.7 %convert_reduce_fusion.3 = (f32[768]{0:T(1024)S(1)}, bf16[512,768]{1,0:T(8,128)(2,1)S(1)}, f32[512,768]{1,0:T(8,128)S(1)}) fusion(f32[512,768]{1,0:T(8,128)S(1)} %convolution_add_fusion.9, bf16[512,768]{1,0:T(8,128)(2,1)S(1)} %copy-done.21, bf16[768,768]{1,0:T(8,128)(2,1)S(1)} %bitcast.264), kind=kOutput, calls=%fused_computation.52 | convolution fusion | flops 633076992 | bytes 5901312 | tf_op jit(solution)/shard_map/dot_general | solution.py:217
  162.2 5.4 %convert_reduce_fusion.2 = (f32[768]{0:T(1024)S(1)}, bf16[512,768]{1,0:T(8,128)(2,1)S(1)}, f32[512,768]{1,0:T(8,128)S(1)}) fusion(f32[512,768]{1,0:T(8,128)S(1)} %convolution_add_fusion.8, bf16[512,768]{1,0:T(8,128)(2,1)S(1)} %copy-done.21, bf16[768,768]{1,0:T(8,128)(2,1)} %collective-permute-done.20), kind=kOutput, calls=%fused_computation.51 | convolution fusion | flops 633076992 | bytes 5901312 | tf_op jit(solution)/shard_map/dot_general | solution.py:217
  167.8 3.9 multiply_convert_fusion.3
  180.0 2.2 fusion.208
  182.3 2.3 fusion.209
  186.6 5.6 %convert_reduce_fusion = (f32[768]{0:T(1024)S(1)}, bf16[512,768]{1,0:T(8,128)(2,1)S(1)}, f32[512,768]{1,0:T(8,128)S(1)}) fusion(f32[512,768]{1,0:T(8,128)S(1)} %convolution_add_fusion.6, bf16[512,768]{1,0:T(8,128)(2,1)S(1)} %copy-done.21, bf16[768,768]{1,0:T(8,128)(2,1)} %collective-permute-done.28), kind=kOutput, calls=%fused_computation.49 | convolution fusion | flops 633076992 | bytes 5901312 | tf_op jit(solution)/shard_map/dot_general | solution.py:217
  193.9 2.7 multiply_reduce_fusion.3
  197.7 2.3 multiply_reduce_fusion.1
  200.1 2.3 convert_reduce_fusion.5
  205.5 13.1 %collective-permute-start.29 = (bf16[208,768]{1,0:T(8,128)(2,1)S(1)}, bf16[208,768]{1,0:T(8,128)(2,1)}, u32[]{:S(2)}, u32[]{:S(2)}) collective-permute-start(bf16[208,768]{1,0:T(8,128)(2,1)S(1)} %get-tuple-element.233), channel_id=1, source_target_pairs={{0,1},{1,2},{2,3},{4,5},{5,6},{6,7},{8,9},{9,10},{10,11},{12,13},{... | collective-permute-start | bytes 958472 | tf_op jit(solution)/shard_map/ppermute | solution.py:460
  219.0 3.1 pad_maximum_fusion.3
  222.2 2.9 convolution_convert_fusion.3
  226.3 2.9 convolution_convert_fusion.2
  231.2 2.9 convolution_convert_fusion.1
  236.1 2.9 convolution_convert_fusion
  246.8 23.4 %attention_backward.1 = (bf16[928,576]{1,0:T(8,128)(2,1)S(1)}, bf16[928,576]{1,0:T(8,128)(2,1)S(1)}, bf16[928,576]{1,0:T(8,128)(2,1)S(1)}, bf16[928,576]{1,0:T(8,128)(2,1)S(1)}) custom-call(s32[8]{0:T(128)S(1)} %stack.202.bounds, bf16[928,768]{1,0:T(8,128)(2,1)S(1)} %add_convert_fusion.3.refs_0_, bf16[928,768]{1,0:T(8,128)(2,1)S(1)} %copy-done.3, ...), custom_call_target="tpu_custom_call" | custom-call | tf_op jit(solution)/shard_map/attention_backward/pallas_call | solution.py:284
  280.5 19.1 %collective-permute-start.56 = (f32[15,768]{1,0:T(8,128)S(1)}, f32[15,768]{1,0:T(8,128)S(1)}, u32[]{:S(2)}, u32[]{:S(2)}) collective-permute-start(f32[15,768]{1,0:T(8,128)S(1)} %concatenate.98), channel_id=1, source_target_pairs={{0,1},{1,0},{2,3},{3,2},{4,5},{5,4},{6,7},{7,6},{8,9},{9,8},{10,11... | collective-permute-start | bytes 138248 | tf_op jit(solution)/shard_map/ppermute | solution.py:39
  299.5 2.3 fusion.142
  301.9 5.7 %collective-permute-start.58 = (f32[15,768]{1,0:T(8,128)S(1)}, f32[15,768]{1,0:T(8,128)}, u32[]{:S(2)}, u32[]{:S(2)}) collective-permute-start(f32[15,768]{1,0:T(8,128)S(1)} %add.747), channel_id=1, source_target_pairs={{0,2},{1,3},{2,0},{3,1},{4,6},{5,7},{6,4},{7,5},{8,10},{9,11},{10,... | collective-permute-start | bytes 138248 | tf_op jit(solution)/shard_map/ppermute | solution.py:39
  307.6 2.3 fusion.139
  309.9 3.2 concatenate.90
  315.6 4.1 concatenate.89
  329.9 3.4 collective-permute-start.61
  336.9 2.4 convolution_add_fusion.11
  345.5 2.3 slice.431
  352.8 2.2 copy.123
  377.2 7.6 %collective-permute-done.41 = bf16[4,2,96,384]{3,2,0,1:T(8,128)(2,1)S(1)} collective-permute-done((bf16[4,2,96,384]{3,2,0,1:T(8,128)(2,1)S(1)}, bf16[4,2,96,384]{3,2,0,1:T(8,128)(2,1)S(1)}, u32[]{:S(2)}, u32[]{:S(2)}) %collective-permute-start.41) | collective-permute-done | bytes 589856 | tf_op jit(solution)/shard_map/ppermute | solution.py:39
  388.0 9.4 %collective-permute-done.49 = bf16[4,2,96,384]{3,2,0,1:T(8,128)(2,1)S(1)} collective-permute-done((bf16[4,2,96,384]{3,2,0,1:T(8,128)(2,1)S(1)}, bf16[4,2,96,384]{3,2,0,1:T(8,128)(2,1)S(1)}, u32[]{:S(2)}, u32[]{:S(2)}) %collective-permute-start.49) | collective-permute-done | bytes 589856 | tf_op jit(solution)/shard_map/ppermute | solution.py:39
  400.7 3.1 collective-permute-done.36
  405.9 4.4 collective-permute-start.39
  410.3 2.7 collective-permute-start.38
  422.4 6.4 %collective-permute-start.55 = (bf16[1,96,768]{2,1,0:T(8,128)(2,1)}, bf16[1,96,768]{2,1,0:T(8,128)(2,1)}, u32[]{:S(2)}, u32[]{:S(2)}) collective-permute-start(bf16[1,96,768]{2,1,0:T(8,128)(2,1)} %get-tuple-element.218), channel_id=1, source_target_pairs={{0,24},{4,28},{8,0},{12,4},{16,8},{20,12},{24,16},{28,20},{1,25},{... | collective-permute-start | bytes 442376 | tf_op jit(solution)/shard_map/ppermute | solution.py:31
  428.8 7.3 %collective-permute-start.54 = (bf16[1,96,768]{2,1,0:T(8,128)(2,1)}, bf16[1,96,768]{2,1,0:T(8,128)(2,1)}, u32[]{:S(2)}, u32[]{:S(2)}) collective-permute-start(bf16[1,96,768]{2,1,0:T(8,128)(2,1)} %get-tuple-element.217), channel_id=1, source_target_pairs={{0,16},{4,20},{8,24},{12,28},{16,0},{20,4},{24,8},{28,12},{1,17},{... | collective-permute-start | bytes 442376 | tf_op jit(solution)/shard_map/ppermute | solution.py:31
  443.2 2.3 fusion.186
  445.5 4.6 %collective-permute-done.53 = bf16[1,96,768]{2,1,0:T(8,128)(2,1)S(1)} collective-permute-done((bf16[1,96,768]{2,1,0:T(8,128)(2,1)S(1)}, bf16[1,96,768]{2,1,0:T(8,128)(2,1)S(1)}, u32[]{:S(2)}, u32[]{:S(2)}) %collective-permute-start.53) | collective-permute-done | bytes 147488 | tf_op jit(solution)/shard_map/ppermute | solution.py:31
  (502 shorter events, 179.6 us)
Async XLA Ops:
  3.1 22.5 %collective-permute-start.2 = (bf16[1,96,768]{2,1,0:T(8,128)(2,1)S(1)}, bf16[1,96,768]{2,1,0:T(8,128)(2,1)S(1)}, u32[]{:S(2)}, u32[]{:S(2)}) collective-permute-start(bf16[1,96,768]{2,1,0:T(8,128)(2,1)S(1)} %get-tuple-element.207), channel_id=1, source_target_pairs={{0,8},{4,12},{8,16},{12,20},{16,24},{20,28},{24,0},{28,4},{1,9},{5... | collective-permute-start | bytes 442376 | tf_op jit(solution)/shard_map/ppermute | solution.py:31
  6.2 19.5 %collective-permute-start.3 = (bf16[1,96,768]{2,1,0:T(8,128)(2,1)S(1)}, bf16[1,96,768]{2,1,0:T(8,128)(2,1)S(1)}, u32[]{:S(2)}, u32[]{:S(2)}) collective-permute-start(bf16[1,96,768]{2,1,0:T(8,128)(2,1)S(1)} %get-tuple-element.207), channel_id=1, source_target_pairs={{0,16},{4,20},{8,24},{12,28},{16,0},{20,4},{24,8},{28,12},{1,17},{... | collective-permute-start | bytes 442376 | tf_op jit(solution)/shard_map/ppermute | solution.py:31
  8.8 16.9 %collective-permute-start.4 = (bf16[1,96,768]{2,1,0:T(8,128)(2,1)S(1)}, bf16[1,96,768]{2,1,0:T(8,128)(2,1)S(1)}, u32[]{:S(2)}, u32[]{:S(2)}) collective-permute-start(bf16[1,96,768]{2,1,0:T(8,128)(2,1)S(1)} %get-tuple-element.207), channel_id=1, source_target_pairs={{0,24},{4,28},{8,0},{12,4},{16,8},{20,12},{24,16},{28,20},{1,25},{... | collective-permute-start | bytes 442376 | tf_op jit(solution)/shard_map/ppermute | solution.py:31
  11.2 33.6 %collective-permute-start.1 = (bf16[208,896]{1,0:T(8,128)(2,1)}, bf16[208,896]{1,0:T(8,128)(2,1)}, u32[]{:S(2)}, u32[]{:S(2)}) collective-permute-start(bf16[208,896]{1,0:T(8,128)(2,1)} %get-tuple-element.232), channel_id=1, source_target_pairs={{1,0},{2,1},{3,2},{5,4},{6,5},{7,6},{9,8},{10,9},{11,10},{13,12},{... | collective-permute-start | bytes 1118216 | tf_op jit(solution)/shard_map/ppermute | solution.py:371
  12.5 33.1 %collective-permute-start = (bf16[208,896]{1,0:T(8,128)(2,1)}, bf16[208,896]{1,0:T(8,128)(2,1)}, u32[]{:S(2)}, u32[]{:S(2)}) collective-permute-start(bf16[208,896]{1,0:T(8,128)(2,1)} %get-tuple-element.231), channel_id=1, source_target_pairs={{0,1},{1,2},{2,3},{4,5},{5,6},{6,7},{8,9},{9,10},{10,11},{12,13},{... | collective-permute-start | bytes 1118216 | tf_op jit(solution)/shard_map/ppermute | solution.py:370
  25.8 39.5 %collective-permute-start.5 = (bf16[4,96,768]{2,1,0:T(8,128)(2,1)S(1)}, bf16[4,96,768]{2,1,0:T(8,128)(2,1)S(1)}, u32[]{:S(2)}, u32[]{:S(2)}) collective-permute-start(bf16[4,96,768]{2,1,0:T(8,128)(2,1)S(1)} %constant_dynamic-update-slice_fusion.8), channel_id=1, source_target_pairs={{0,4},{4,0},{8,12},{12,8},{16,20},{20,16},{24,28},{28,24},{1,5},{5... | collective-permute-start | bytes 1769480 | tf_op jit(solution)/shard_map/ppermute | solution.py:31
  28.0 13.4 %collective-permute-start.12 = (bf16[1,96,768]{2,1,0:T(8,128)(2,1)S(1)}, bf16[1,96,768]{2,1,0:T(8,128)(2,1)S(1)}, u32[]{:S(2)}, u32[]{:S(2)}) collective-permute-start(bf16[1,96,768]{2,1,0:T(8,128)(2,1)S(1)} %bitcast.276), channel_id=1, source_target_pairs={{0,16},{4,20},{8,24},{12,28},{16,0},{20,4},{24,8},{28,12},{1,17},{... | collective-permute-start | bytes 442376 | tf_op jit(solution)/shard_map/ppermute | solution.py:31
  41.5 16.1 %collective-permute-start.8 = (bf16[4,96,384]{2,1,0:T(8,128)(2,1)S(1)}, bf16[4,96,384]{2,1,0:T(8,128)(2,1)S(1)}, u32[]{:S(2)}, u32[]{:S(2)}) collective-permute-start(bf16[4,96,384]{2,1,0:T(8,128)(2,1)S(1)} %slice.325), channel_id=1, source_target_pairs={{0,2},{1,3},{2,0},{3,1},{4,6},{5,7},{6,4},{7,5},{8,10},{9,11},{10,... | collective-permute-start | bytes 884744 | tf_op jit(solution)/shard_map/ppermute | solution.py:39
  55.3 37.1 %collective-permute-start.14 = (bf16[4,96,768]{2,1,0:T(8,128)(2,1)S(1)}, bf16[4,96,768]{2,1,0:T(8,128)(2,1)S(1)}, u32[]{:S(2)}, u32[]{:S(2)}) collective-permute-start(bf16[4,96,768]{2,1,0:T(8,128)(2,1)S(1)} %constant_dynamic-update-slice_fusion.4), channel_id=1, source_target_pairs={{0,4},{4,0},{8,12},{12,8},{16,20},{20,16},{24,28},{28,24},{1,5},{5... | collective-permute-start | bytes 1769480 | tf_op jit(solution)/shard_map/ppermute | solution.py:31
  56.0 37.4 %collective-permute-start.18 = (bf16[4,96,768]{2,1,0:T(8,128)(2,1)S(1)}, bf16[4,96,768]{2,1,0:T(8,128)(2,1)S(1)}, u32[]{:S(2)}, u32[]{:S(2)}) collective-permute-start(bf16[4,96,768]{2,1,0:T(8,128)(2,1)S(1)} %constant_dynamic-update-slice_fusion), channel_id=1, source_target_pairs={{0,4},{4,0},{8,12},{12,8},{16,20},{20,16},{24,28},{28,24},{1,5},{5... | collective-permute-start | bytes 1769480 | tf_op jit(solution)/shard_map/ppermute | solution.py:31
  57.6 33.2 %collective-permute-start.25 = (bf16[4,96,384]{2,1,0:T(8,128)(2,1)S(1)}, bf16[4,96,384]{2,1,0:T(8,128)(2,1)S(1)}, u32[]{:S(2)}, u32[]{:S(2)}) collective-permute-start(bf16[4,96,384]{2,1,0:T(8,128)(2,1)S(1)} %slice.414), channel_id=1, source_target_pairs={{0,2},{1,3},{2,0},{3,1},{4,6},{5,7},{6,4},{7,5},{8,10},{9,11},{10,... | collective-permute-start | bytes 884744 | tf_op jit(solution)/shard_map/ppermute | solution.py:39
  64.7 25.8 %collective-permute-start.9 = (bf16[4,96,384]{2,1,0:T(8,128)(2,1)S(1)}, bf16[4,96,384]{2,1,0:T(8,128)(2,1)S(1)}, u32[]{:S(2)}, u32[]{:S(2)}) collective-permute-start(bf16[4,96,384]{2,1,0:T(8,128)(2,1)S(1)} %collective-permute-done.8), channel_id=1, source_target_pairs={{0,4},{4,0},{8,12},{12,8},{16,20},{20,16},{24,28},{28,24},{1,5},{5... | collective-permute-start | bytes 884744 | tf_op jit(solution)/shard_map/ppermute | solution.py:31
  65.3 30.9 %collective-permute-start.23 = (bf16[4,96,384]{2,1,0:T(8,128)(2,1)S(1)}, bf16[4,96,384]{2,1,0:T(8,128)(2,1)S(1)}, u32[]{:S(2)}, u32[]{:S(2)}) collective-permute-start(bf16[4,96,384]{2,1,0:T(8,128)(2,1)S(1)} %collective-permute-done.22), channel_id=1, source_target_pairs={{0,4},{4,0},{8,12},{12,8},{16,20},{20,16},{24,28},{28,24},{1,5},{5... | collective-permute-start | bytes 884744 | tf_op jit(solution)/shard_map/ppermute | solution.py:31
  90.5 42.6 %collective-permute-start.6 = (bf16[768,768]{1,0:T(8,128)(2,1)S(1)}, bf16[768,768]{1,0:T(8,128)(2,1)S(1)}, u32[]{:S(2)}, u32[]{:S(2)}) collective-permute-start(bf16[768,768]{1,0:T(8,128)(2,1)S(1)} %bitcast.243), channel_id=1, source_target_pairs={{0,1},{1,0},{2,3},{3,2},{4,5},{5,4},{6,7},{7,6},{8,9},{9,8},{10,11... | collective-permute-start | bytes 3538952 | tf_op jit(solution)/shard_map/ppermute | solution.py:39
  90.8 16.2 %collective-permute-start.7 = (bf16[768,384]{1,0:T(8,128)(2,1)S(1)}, bf16[768,384]{1,0:T(8,128)(2,1)S(1)}, u32[]{:S(2)}, u32[]{:S(2)}) collective-permute-start(bf16[768,384]{1,0:T(8,128)(2,1)S(1)} %slice.407), channel_id=1, source_target_pairs={{0,2},{1,3},{2,0},{3,1},{4,6},{5,7},{6,4},{7,5},{8,10},{9,11},{10,... | collective-permute-start | bytes 1769480 | tf_op jit(solution)/shard_map/ppermute | solution.py:39
  93.4 65.5 %collective-permute-start.19 = (bf16[768,768]{1,0:T(8,128)(2,1)S(1)}, bf16[768,768]{1,0:T(8,128)(2,1)S(1)}, u32[]{:S(2)}, u32[]{:S(2)}) collective-permute-start(bf16[768,768]{1,0:T(8,128)(2,1)S(1)} %bitcast.259), channel_id=1, source_target_pairs={{0,1},{1,0},{2,3},{3,2},{4,5},{5,4},{6,7},{7,6},{8,9},{9,8},{10,11... | collective-permute-start | bytes 3538952 | tf_op jit(solution)/shard_map/ppermute | solution.py:39
  96.1 23.5 %collective-permute-start.21 = (bf16[768,384]{1,0:T(8,128)(2,1)S(1)}, bf16[768,384]{1,0:T(8,128)(2,1)S(1)}, u32[]{:S(2)}, u32[]{:S(2)}) collective-permute-start(bf16[768,384]{1,0:T(8,128)(2,1)S(1)} %slice.412), channel_id=1, source_target_pairs={{0,2},{1,3},{2,0},{3,1},{4,6},{5,7},{6,4},{7,5},{8,10},{9,11},{10,... | collective-permute-start | bytes 1769480 | tf_op jit(solution)/shard_map/ppermute | solution.py:39
  107.1 27.8 %collective-permute-start.10 = (bf16[768,768]{1,0:T(8,128)(2,1)S(1)}, bf16[768,768]{1,0:T(8,128)(2,1)S(1)}, u32[]{:S(2)}, u32[]{:S(2)}) collective-permute-start(bf16[768,768]{1,0:T(8,128)(2,1)S(1)} %pad_maximum_fusion.8), channel_id=1, source_target_pairs={{0,1},{1,0},{2,3},{3,2},{4,5},{5,4},{6,7},{7,6},{8,9},{9,8},{10,11... | collective-permute-start | bytes 3538952 | tf_op jit(solution)/shard_map/ppermute | solution.py:39
  107.5 24.4 %collective-permute-start.24 = (bf16[768,384]{1,0:T(8,128)(2,1)S(1)}, bf16[768,384]{1,0:T(8,128)(2,1)S(1)}, u32[]{:S(2)}, u32[]{:S(2)}) collective-permute-start(bf16[768,384]{1,0:T(8,128)(2,1)S(1)} %slice.413), channel_id=1, source_target_pairs={{0,2},{1,3},{2,0},{3,1},{4,6},{5,7},{6,4},{7,5},{8,10},{9,11},{10,... | collective-permute-start | bytes 1769480 | tf_op jit(solution)/shard_map/ppermute | solution.py:39
  119.6 42.6 %collective-permute-start.20 = (bf16[768,768]{1,0:T(8,128)(2,1)S(1)}, bf16[768,768]{1,0:T(8,128)(2,1)}, u32[]{:S(2)}, u32[]{:S(2)}) collective-permute-start(bf16[768,768]{1,0:T(8,128)(2,1)S(1)} %bitcast.263), channel_id=1, source_target_pairs={{0,1},{1,0},{2,3},{3,2},{4,5},{5,4},{6,7},{7,6},{8,9},{9,8},{10,11... | collective-permute-start | bytes 3538952 | tf_op jit(solution)/shard_map/ppermute | solution.py:39
  131.9 52.7 %collective-permute-start.27 = (bf16[768,768]{1,0:T(8,128)(2,1)}, bf16[768,768]{1,0:T(8,128)(2,1)}, u32[]{:S(2)}, u32[]{:S(2)}) collective-permute-start(bf16[768,768]{1,0:T(8,128)(2,1)} %pad_maximum_fusion.12), channel_id=1, source_target_pairs={{0,1},{1,0},{2,3},{3,2},{4,5},{5,4},{6,7},{7,6},{8,9},{9,8},{10,11... | collective-permute-start | bytes 3538952 | tf_op jit(solution)/shard_map/ppermute | solution.py:39
  133.1 53.5 %collective-permute-start.28 = (bf16[768,768]{1,0:T(8,128)(2,1)}, bf16[768,768]{1,0:T(8,128)(2,1)}, u32[]{:S(2)}, u32[]{:S(2)}) collective-permute-start(bf16[768,768]{1,0:T(8,128)(2,1)} %pad_maximum_fusion.13), channel_id=1, source_target_pairs={{0,1},{1,0},{2,3},{3,2},{4,5},{5,4},{6,7},{7,6},{8,9},{9,8},{10,11... | collective-permute-start | bytes 3538952 | tf_op jit(solution)/shard_map/ppermute | solution.py:39
  204.2 17.9 %collective-permute-start.30 = (bf16[208,768]{1,0:T(8,128)(2,1)}, bf16[208,768]{1,0:T(8,128)(2,1)}, u32[]{:S(2)}, u32[]{:S(2)}) collective-permute-start(bf16[208,768]{1,0:T(8,128)(2,1)} %get-tuple-element.234), channel_id=1, source_target_pairs={{1,0},{2,1},{3,2},{5,4},{6,5},{7,6},{9,8},{10,9},{11,10},{13,12},{... | collective-permute-start | bytes 958472 | tf_op jit(solution)/shard_map/ppermute | solution.py:461
  205.5 16.6 %collective-permute-start.29 = (bf16[208,768]{1,0:T(8,128)(2,1)S(1)}, bf16[208,768]{1,0:T(8,128)(2,1)}, u32[]{:S(2)}, u32[]{:S(2)}) collective-permute-start(bf16[208,768]{1,0:T(8,128)(2,1)S(1)} %get-tuple-element.233), channel_id=1, source_target_pairs={{0,1},{1,2},{2,3},{4,5},{5,6},{6,7},{8,9},{9,10},{10,11},{12,13},{... | collective-permute-start | bytes 958472 | tf_op jit(solution)/shard_map/ppermute | solution.py:460
  280.5 21.4 %collective-permute-start.56 = (f32[15,768]{1,0:T(8,128)S(1)}, f32[15,768]{1,0:T(8,128)S(1)}, u32[]{:S(2)}, u32[]{:S(2)}) collective-permute-start(f32[15,768]{1,0:T(8,128)S(1)} %concatenate.98), channel_id=1, source_target_pairs={{0,1},{1,0},{2,3},{3,2},{4,5},{5,4},{6,7},{7,6},{8,9},{9,8},{10,11... | collective-permute-start | bytes 138248 | tf_op jit(solution)/shard_map/ppermute | solution.py:39
  301.9 18.0 %collective-permute-start.58 = (f32[15,768]{1,0:T(8,128)S(1)}, f32[15,768]{1,0:T(8,128)}, u32[]{:S(2)}, u32[]{:S(2)}) collective-permute-start(f32[15,768]{1,0:T(8,128)S(1)} %add.747), channel_id=1, source_target_pairs={{0,2},{1,3},{2,0},{3,1},{4,6},{5,7},{6,4},{7,5},{8,10},{9,11},{10,... | collective-permute-start | bytes 138248 | tf_op jit(solution)/shard_map/ppermute | solution.py:39
  313.1 23.7 %collective-permute-start.32 = (bf16[512,1152]{1,0:T(8,128)(2,1)}, bf16[512,1152]{1,0:T(8,128)(2,1)}, u32[]{:S(2)}, u32[]{:S(2)}) collective-permute-start(bf16[512,1152]{1,0:T(8,128)(2,1)} %concatenate.90), channel_id=1, source_target_pairs={{0,1},{1,0},{2,3},{3,2},{4,5},{5,4},{6,7},{7,6},{8,9},{9,8},{10,11... | collective-permute-start | bytes 3538952 | tf_op jit(solution)/shard_map/ppermute | solution.py:39
  313.3 44.8 %collective-permute-start.40 = (bf16[512,2304]{1,0:T(8,128)(2,1)}, bf16[512,2304]{1,0:T(8,128)(2,1)}, u32[]{:S(2)}, u32[]{:S(2)}) collective-permute-start(bf16[512,2304]{1,0:T(8,128)(2,1)} %pad_maximum_fusion.2), channel_id=1, source_target_pairs={{0,1},{1,0},{2,3},{3,2},{4,5},{5,4},{6,7},{7,6},{8,9},{9,8},{10,11... | collective-permute-start | bytes 7077896 | tf_op jit(solution)/shard_map/ppermute | solution.py:39
  319.7 21.3 %collective-permute-start.31 = (bf16[512,1920]{1,0:T(8,128)(2,1)}, bf16[512,1920]{1,0:T(8,128)(2,1)S(1)}, u32[]{:S(2)}, u32[]{:S(2)}) collective-permute-start(bf16[512,1920]{1,0:T(8,128)(2,1)} %concatenate.89), channel_id=1, source_target_pairs={{0,1},{1,0},{2,3},{3,2},{4,5},{5,4},{6,7},{7,6},{8,9},{9,8},{10,11... | collective-permute-start | bytes 5898248 | tf_op jit(solution)/shard_map/ppermute | solution.py:39
  324.4 36.2 %collective-permute-start.48 = (bf16[512,2304]{1,0:T(8,128)(2,1)}, bf16[512,2304]{1,0:T(8,128)(2,1)}, u32[]{:S(2)}, u32[]{:S(2)}) collective-permute-start(bf16[512,2304]{1,0:T(8,128)(2,1)} %pad_maximum_fusion.3), channel_id=1, source_target_pairs={{0,1},{1,0},{2,3},{3,2},{4,5},{5,4},{6,7},{7,6},{8,9},{9,8},{10,11... | collective-permute-start | bytes 7077896 | tf_op jit(solution)/shard_map/ppermute | solution.py:39
  356.1 18.6 %collective-permute-start.33 = (bf16[4,2,96,384]{3,2,0,1:T(8,128)(2,1)S(1)}, bf16[4,2,96,384]{3,2,0,1:T(8,128)(2,1)S(1)}, u32[]{:S(2)}, u32[]{:S(2)}) collective-permute-start(bf16[4,2,96,384]{3,2,0,1:T(8,128)(2,1)S(1)} %copy.197), channel_id=1, source_target_pairs={{0,2},{1,3},{2,0},{3,1},{4,6},{5,7},{6,4},{7,5},{8,10},{9,11},{10,... | collective-permute-start | bytes 1769480 | tf_op jit(solution)/shard_map/ppermute | solution.py:39
  356.7 19.4 %collective-permute-start.35 = (bf16[2,4,96,384]{3,2,1,0:T(8,128)(2,1)S(1)}, bf16[2,4,96,384]{3,2,1,0:T(8,128)(2,1)S(1)}, u32[]{:S(2)}, u32[]{:S(2)}) collective-permute-start(bf16[2,4,96,384]{3,2,1,0:T(8,128)(2,1)S(1)} %pad_maximum_fusion.17), channel_id=1, source_target_pairs={{0,4},{4,0},{8,12},{12,8},{16,20},{20,16},{24,28},{28,24},{1,5},{5... | collective-permute-start | bytes 1769480 | tf_op jit(solution)/shard_map/ppermute | solution.py:31
  368.4 16.3 %collective-permute-start.41 = (bf16[4,2,96,384]{3,2,0,1:T(8,128)(2,1)S(1)}, bf16[4,2,96,384]{3,2,0,1:T(8,128)(2,1)S(1)}, u32[]{:S(2)}, u32[]{:S(2)}) collective-permute-start(bf16[4,2,96,384]{3,2,0,1:T(8,128)(2,1)S(1)} %copy.196), channel_id=1, source_target_pairs={{0,2},{1,3},{2,0},{3,1},{4,6},{5,7},{6,4},{7,5},{8,10},{9,11},{10,... | collective-permute-start | bytes 1769480 | tf_op jit(solution)/shard_map/ppermute | solution.py:39
  370.4 16.3 %collective-permute-start.43 = (bf16[2,4,96,384]{3,2,1,0:T(8,128)(2,1)S(1)}, bf16[2,4,96,384]{3,2,1,0:T(8,128)(2,1)S(1)}, u32[]{:S(2)}, u32[]{:S(2)}) collective-permute-start(bf16[2,4,96,384]{3,2,1,0:T(8,128)(2,1)S(1)} %pad_maximum_fusion.18), channel_id=1, source_target_pairs={{0,4},{4,0},{8,12},{12,8},{16,20},{20,16},{24,28},{28,24},{1,5},{5... | collective-permute-start | bytes 1769480 | tf_op jit(solution)/shard_map/ppermute | solution.py:31
  371.7 25.7 %collective-permute-start.49 = (bf16[4,2,96,384]{3,2,0,1:T(8,128)(2,1)S(1)}, bf16[4,2,96,384]{3,2,0,1:T(8,128)(2,1)S(1)}, u32[]{:S(2)}, u32[]{:S(2)}) collective-permute-start(bf16[4,2,96,384]{3,2,0,1:T(8,128)(2,1)S(1)} %copy.195), channel_id=1, source_target_pairs={{0,2},{1,3},{2,0},{3,1},{4,6},{5,7},{6,4},{7,5},{8,10},{9,11},{10,... | collective-permute-start | bytes 1769480 | tf_op jit(solution)/shard_map/ppermute | solution.py:39
  374.8 24.7 %collective-permute-start.51 = (bf16[2,4,96,384]{3,2,1,0:T(8,128)(2,1)S(1)}, bf16[2,4,96,384]{3,2,1,0:T(8,128)(2,1)S(1)}, u32[]{:S(2)}, u32[]{:S(2)}) collective-permute-start(bf16[2,4,96,384]{3,2,1,0:T(8,128)(2,1)S(1)} %pad_maximum_fusion.19), channel_id=1, source_target_pairs={{0,4},{4,0},{8,12},{12,8},{16,20},{20,16},{24,28},{28,24},{1,5},{5... | collective-permute-start | bytes 1769480 | tf_op jit(solution)/shard_map/ppermute | solution.py:31
  376.0 29.7 %collective-permute-start.34 = (bf16[4,96,384]{2,1,0:T(8,128)(2,1)S(1)}, bf16[4,96,384]{2,1,0:T(8,128)(2,1)S(1)}, u32[]{:S(2)}, u32[]{:S(2)}) collective-permute-start(bf16[4,96,384]{2,1,0:T(8,128)(2,1)S(1)} %fusion.93), channel_id=1, source_target_pairs={{0,4},{4,0},{8,12},{12,8},{16,20},{20,16},{24,28},{28,24},{1,5},{5... | collective-permute-start | bytes 884744 | tf_op jit(solution)/shard_map/ppermute | solution.py:31
  384.8 19.0 %collective-permute-start.36 = (bf16[4,96,384]{2,1,0:T(8,128)(2,1)S(1)}, bf16[4,96,384]{2,1,0:T(8,128)(2,1)S(1)}, u32[]{:S(2)}, u32[]{:S(2)}) collective-permute-start(bf16[4,96,384]{2,1,0:T(8,128)(2,1)S(1)} %fusion.59), channel_id=1, source_target_pairs={{0,2},{1,3},{2,0},{3,1},{4,6},{5,7},{6,4},{7,5},{8,10},{9,11},{10,... | collective-permute-start | bytes 884744 | tf_op jit(solution)/shard_map/ppermute | solution.py:39
  386.8 26.3 %collective-permute-start.42 = (bf16[4,96,384]{2,1,0:T(8,128)(2,1)S(1)}, bf16[4,96,384]{2,1,0:T(8,128)(2,1)S(1)}, u32[]{:S(2)}, u32[]{:S(2)}) collective-permute-start(bf16[4,96,384]{2,1,0:T(8,128)(2,1)S(1)} %fusion.95), channel_id=1, source_target_pairs={{0,4},{4,0},{8,12},{12,8},{16,20},{20,16},{24,28},{28,24},{1,5},{5... | collective-permute-start | bytes 884744 | tf_op jit(solution)/shard_map/ppermute | solution.py:31
  397.4 12.9 %collective-permute-start.44 = (bf16[4,96,384]{2,1,0:T(8,128)(2,1)S(1)}, bf16[4,96,384]{2,1,0:T(8,128)(2,1)S(1)}, u32[]{:S(2)}, u32[]{:S(2)}) collective-permute-start(bf16[4,96,384]{2,1,0:T(8,128)(2,1)S(1)} %fusion.57), channel_id=1, source_target_pairs={{0,2},{1,3},{2,0},{3,1},{4,6},{5,7},{6,4},{7,5},{8,10},{9,11},{10,... | collective-permute-start | bytes 884744 | tf_op jit(solution)/shard_map/ppermute | solution.py:39
  399.4 18.5 %collective-permute-start.50 = (bf16[4,96,384]{2,1,0:T(8,128)(2,1)S(1)}, bf16[4,96,384]{2,1,0:T(8,128)(2,1)S(1)}, u32[]{:S(2)}, u32[]{:S(2)}) collective-permute-start(bf16[4,96,384]{2,1,0:T(8,128)(2,1)S(1)} %fusion.96), channel_id=1, source_target_pairs={{0,4},{4,0},{8,12},{12,8},{16,20},{20,16},{24,28},{28,24},{1,5},{5... | collective-permute-start | bytes 884744 | tf_op jit(solution)/shard_map/ppermute | solution.py:31
  405.9 13.0 %collective-permute-start.39 = (bf16[1,96,768]{2,1,0:T(8,128)(2,1)S(1)}, bf16[1,96,768]{2,1,0:T(8,128)(2,1)S(1)}, u32[]{:S(2)}, u32[]{:S(2)}) collective-permute-start(bf16[1,96,768]{2,1,0:T(8,128)(2,1)S(1)} %get-tuple-element.224), channel_id=1, source_target_pairs={{0,24},{4,28},{8,0},{12,4},{16,8},{20,12},{24,16},{28,20},{1,25},{... | collective-permute-start | bytes 442376 | tf_op jit(solution)/shard_map/ppermute | solution.py:31
  413.1 15.7 %collective-permute-start.37 = (bf16[1,96,768]{2,1,0:T(8,128)(2,1)S(1)}, bf16[1,96,768]{2,1,0:T(8,128)(2,1)S(1)}, u32[]{:S(2)}, u32[]{:S(2)}) collective-permute-start(bf16[1,96,768]{2,1,0:T(8,128)(2,1)S(1)} %get-tuple-element.222), channel_id=1, source_target_pairs={{0,8},{4,12},{8,16},{12,20},{16,24},{20,28},{24,0},{28,4},{1,9},{5... | collective-permute-start | bytes 442376 | tf_op jit(solution)/shard_map/ppermute | solution.py:31
  416.0 27.0 %collective-permute-start.47 = (bf16[1,96,768]{2,1,0:T(8,128)(2,1)}, bf16[1,96,768]{2,1,0:T(8,128)(2,1)}, u32[]{:S(2)}, u32[]{:S(2)}) collective-permute-start(bf16[1,96,768]{2,1,0:T(8,128)(2,1)} %get-tuple-element.221), channel_id=1, source_target_pairs={{0,24},{4,28},{8,0},{12,4},{16,8},{20,12},{24,16},{28,20},{1,25},{... | collective-permute-start | bytes 442376 | tf_op jit(solution)/shard_map/ppermute | solution.py:31
  418.0 25.2 %collective-permute-start.46 = (bf16[1,96,768]{2,1,0:T(8,128)(2,1)}, bf16[1,96,768]{2,1,0:T(8,128)(2,1)}, u32[]{:S(2)}, u32[]{:S(2)}) collective-permute-start(bf16[1,96,768]{2,1,0:T(8,128)(2,1)} %get-tuple-element.220), channel_id=1, source_target_pairs={{0,16},{4,20},{8,24},{12,28},{16,0},{20,4},{24,8},{28,12},{1,17},{... | collective-permute-start | bytes 442376 | tf_op jit(solution)/shard_map/ppermute | solution.py:31
  418.9 24.2 %collective-permute-start.45 = (bf16[1,96,768]{2,1,0:T(8,128)(2,1)}, bf16[1,96,768]{2,1,0:T(8,128)(2,1)}, u32[]{:S(2)}, u32[]{:S(2)}) collective-permute-start(bf16[1,96,768]{2,1,0:T(8,128)(2,1)} %get-tuple-element.219), channel_id=1, source_target_pairs={{0,8},{4,12},{8,16},{12,20},{16,24},{20,28},{24,0},{28,4},{1,9},{5... | collective-permute-start | bytes 442376 | tf_op jit(solution)/shard_map/ppermute | solution.py:31
  422.4 23.1 %collective-permute-start.55 = (bf16[1,96,768]{2,1,0:T(8,128)(2,1)}, bf16[1,96,768]{2,1,0:T(8,128)(2,1)}, u32[]{:S(2)}, u32[]{:S(2)}) collective-permute-start(bf16[1,96,768]{2,1,0:T(8,128)(2,1)} %get-tuple-element.218), channel_id=1, source_target_pairs={{0,24},{4,28},{8,0},{12,4},{16,8},{20,12},{24,16},{28,20},{1,25},{... | collective-permute-start | bytes 442376 | tf_op jit(solution)/shard_map/ppermute | solution.py:31
  428.8 16.7 %collective-permute-start.54 = (bf16[1,96,768]{2,1,0:T(8,128)(2,1)}, bf16[1,96,768]{2,1,0:T(8,128)(2,1)}, u32[]{:S(2)}, u32[]{:S(2)}) collective-permute-start(bf16[1,96,768]{2,1,0:T(8,128)(2,1)} %get-tuple-element.217), channel_id=1, source_target_pairs={{0,16},{4,20},{8,24},{12,28},{16,0},{20,4},{24,8},{28,12},{1,17},{... | collective-permute-start | bytes 442376 | tf_op jit(solution)/shard_map/ppermute | solution.py:31
  (103 other events, 963.6 us)
